TPU v7x, 128 devices: a whole 4x4x4 slice. The times are simulated.
128 devices in a mesh: leaf: 32 (over y, x, core), sub: 4 (over z).
Axes of the slice: x: 4, y: 4, z: 4, core: 2. Of those that a mesh axis runs over, the one named last changes fastest.
Arguments:
- charges: float32 [16, 64, 4, 32, 2048], P(None, None, 'sub', 'leaf'), may hold values from -6 to 6
- ordering: int32 [4, 32, 2048], P('sub', 'leaf'), may hold values from 0 to 2047, each once within a row
- jitter: float32 [3, 4, 32, 2048], P(None, 'sub', 'leaf'), may hold values from 0 to 1
- leaf_bases: float32 [4, 32, 64, 2048], P('sub', 'leaf'), may hold values from -0.125 to 0.125
- transfer: float32 [7, 2, 64, 64], replicated, may hold values from -0.5 to 0.5
- coupling: float32 [7, 2, 64, 64], replicated, may hold values from -0.75 to 0.75
Outputs:
- potential: float32 [16, 64, 4, 32, 2048], P(None, None, 'sub', 'leaf')
All inputs are finite; a program needn't handle non-finite values.
Results may differ from a plain program's by a relative error of at most 0.0003.
Values sent between devices are 32-bit elements; how exact they have to be, the bound alone decides.
A program may use at most 128 MiB of HBM per device.

v0:
```python
import jax
import jax.numpy as jnp
from jax import lax
from jax.experimental import pallas as pl
from jax.experimental.pallas import tpu as pltpu
from jax.sharding import PartitionSpec as P

DELTA_SQ = 0.0025
PRECISE = lax.Precision.HIGHEST
F8 = jnp.float8_e4m3fn
BF = jnp.bfloat16
F32 = jnp.float32
GAIN = 16.0
TOP = 384.0
FEATS = 32
SUB = 256
LIMIT = 60 * 1024 * 1024


def swapped(value, axis, stride):
    mask = 2**stride
    pairs = [(source, source ^ mask) for source in range(lax.axis_size(axis))]
    return lax.ppermute(value, axis, pairs)


def lift_pair(current, sibling, branch_bit, transfer_pair):
    left_part = jnp.where(branch_bit == 0, current, sibling)
    right_part = jnp.where(branch_bit == 0, sibling, current)
    parent = jnp.dot(
        left_part, transfer_pair[0], precision=PRECISE, preferred_element_type=jnp.float32
    )
    return parent + jnp.dot(
        right_part, transfer_pair[1], precision=PRECISE, preferred_element_type=jnp.float32
    )


def contract_last(left_mat, right_mat):
    return lax.dot_general(
        left_mat,
        right_mat,
        (((1,), (1,)), ((), ())),
        precision=PRECISE,
        preferred_element_type=jnp.float32,
    )


def mm(left, right):
    return jnp.dot(left, right, preferred_element_type=F32)


def mm_nt(left, right):
    return lax.dot_general(left, right, (((1,), (1,)), ((), ())), preferred_element_type=F32)


def rounded(value):
    return lax.reduce_precision(value, 8, 7)


def pieces(value):
    high = rounded(value)
    middle = rounded(value - high)
    return high, middle, rounded(value - high - middle)


def features(coords):
    parts = [pieces(coords[axis]) for axis in range(3)]
    norm = jnp.sum(coords * coords, axis=0)
    ones = jnp.ones_like(norm)
    source = []
    target = []
    for part in parts:
        for left, right in ((0, 0), (0, 1), (1, 0), (1, 1), (0, 2), (2, 0)):
            source.append(part[left])
            target.append(-2.0 * part[right])
    softened = norm + DELTA_SQ / (GAIN * GAIN)
    source += list(pieces(softened)) + [ones] * 3
    target += [ones] * 3 + list(pieces(norm))
    blank = [jnp.zeros_like(norm)] * (FEATS - len(source))
    return jnp.stack(source + blank).astype(BF), jnp.stack(target + blank).astype(BF)


def scaled(rows):
    top = jnp.maximum(jnp.max(jnp.abs(rows), axis=1, keepdims=True), 1e-30)
    full = rows * (TOP / top)
    high = full.astype(BF)
    return full, high, full - high.astype(F32), top * (1.0 / TOP)


def prepare_kernel(
    q_ref, order_ref, x_ref, qh_ref, q8h_ref, q8l_ref, unit_ref, tail_ref, head_ref, moment_ref,
    feat_ref, pick, pick8, basis,
):
    points = q_ref.shape[1]
    strip = tail_ref.shape[1]
    rank = moment_ref.shape[1]

    @pl.when(pl.program_id(0) == 0)
    def _():
        @pl.loop(0, points // SUB)
        def _(step):
            rows = pl.ds(pl.multiple_of(step * SUB, SUB), SUB)
            own = lax.broadcasted_iota(jnp.int32, (SUB, strip), 0) + step * SUB
            for part in range(points // strip):
                columns = slice(part * strip, (part + 1) * strip)
                hit = jnp.where(own == order_ref[:, columns], 1.0, 0.0)
                pick[rows, columns] = hit.astype(BF)
                if part == 0:
                    pick8[rows, :strip] = hit.astype(F8)
                if part == points // strip - 1:
                    pick8[rows, strip:] = hit.astype(F8)
            moved = mm_nt(pick[rows, :], x_ref[...]).astype(BF)
            feat_ref[rows, :] = moved[:, 2 * rank :]
            basis[rows, :] = moved[:, : 2 * rank]

    full, high, rest, unit = scaled(q_ref[...])
    low8 = rest.astype(F8)
    qh_ref[...] = high
    q8h_ref[...] = full.astype(F8)
    q8l_ref[...] = low8
    unit_ref[...] = jnp.broadcast_to(unit, unit_ref.shape)
    head_ref[...] = (mm(high, pick[:, :strip]) + mm(low8, pick8[:, :strip])) * unit
    last = points - strip
    tail_ref[...] = (mm(high, pick[:, last:]) + mm(low8, pick8[:, strip:])) * unit
    both = mm(high, basis[...])
    moment_ref[...] = (
        both[:, :rank] + both[:, rank:] + mm(rest.astype(BF), basis[:, :rank])
    ) * unit


def prepare(charges, order, stacked):
    rows, points = charges.shape
    strip = points // 4
    rank = (stacked.shape[0] - FEATS) // 2
    chunk = 256
    whole = lambda shape: pl.BlockSpec(shape, lambda step: (0, 0))
    sliced = lambda width: pl.BlockSpec((chunk, width), lambda step: (step, 0))
    shape = jax.ShapeDtypeStruct
    return pl.pallas_call(
        prepare_kernel,
        grid=(rows // chunk,),
        in_specs=[sliced(points), whole(order.shape), whole(stacked.shape)],
        out_specs=[sliced(points)] * 3
        + [sliced(128), sliced(strip), sliced(strip), sliced(rank), whole((points, FEATS))],
        out_shape=[
            shape((rows, points), BF),
            shape((rows, points), F8),
            shape((rows, points), F8),
            shape((rows, 128), F32),
            shape((rows, strip), F32),
            shape((rows, strip), F32),
            shape((rows, rank), F32),
            shape((points, FEATS), BF),
        ],
        scratch_shapes=[
            pltpu.VMEM((points, points), BF),
            pltpu.VMEM((points, 2 * strip), F8),
            pltpu.VMEM((points, 2 * rank), BF),
        ],
        compiler_params=pltpu.CompilerParams(vmem_limit_bytes=LIMIT),
        cost_estimate=pl.CostEstimate(
            flops=14_000_000_000, bytes_accessed=28_000_000, transcendentals=0
        ),
        name="prepare",
    )(charges, order, stacked)


def weigh(source_ref, target, first, last, slot, w, w8h, w8l):
    for row in range(first, last, 128):
        rows = slice(row, row + 128)
        weight = lax.rsqrt(mm(source_ref[rows, :], target))
        high = weight.astype(BF)
        w[slot, rows, :] = high
        w8h[slot, rows, :] = weight.astype(F8)
        w8l[slot, rows, :] = (weight - high.astype(F32)).astype(F8)


def sweep(source_ref, target_ref, row_count, w, w8h, w8l, emit):
    points = source_ref.shape[0]
    blocks = target_ref.shape[1] // SUB
    step = pl.program_id(0)
    parts = 4

    def target(block):
        return target_ref[:, pl.ds(pl.multiple_of(block * SUB, SUB), SUB)]

    @pl.when(step == 0)
    def _():
        weigh(source_ref, target(0), 0, points, 0, w, w8h, w8l)

    for slot in range(2):
        coming = target(jnp.minimum(2 * step + slot + 1, blocks - 1))
        for part in range(parts):
            count = row_count // parts
            weigh(
                source_ref,
                coming,
                part * points // parts,
                (part + 1) * points // parts,
                1 - slot,
                w,
                w8h,
                w8l,
            )
            emit(slice(part * count, (part + 1) * count), slot)


def own_kernel(qh_ref, q8h_ref, q8l_ref, unit_ref, source_ref, target_ref, out_ref, w, w8h, w8l):
    def emit(rows, slot):
        total = mm(qh_ref[rows, :], w[slot])
        total = total + mm(q8h_ref[rows, :], w8l[slot])
        total = total + mm(q8l_ref[rows, :], w8h[slot])
        out_ref[rows, slot * SUB : (slot + 1) * SUB] = total * unit_ref[rows, 0:1]

    sweep(source_ref, target_ref, out_ref.shape[0], w, w8h, w8l, emit)


def weight_scratch(count):
    return [
        pltpu.VMEM((2, count, SUB), BF),
        pltpu.VMEM((2, count, SUB), F8),
        pltpu.VMEM((2, count, SUB), F8),
    ]


def own_near(high, high8, low8, unit, source, target):
    rows, points = high.shape
    whole = lambda a: pl.BlockSpec(a.shape, lambda step: (0, 0), pipeline_mode=pl.Buffered(1))
    return pl.pallas_call(
        own_kernel,
        grid=(points // (2 * SUB),),
        in_specs=[whole(a) for a in (high, high8, low8, unit, source, target)],
        out_specs=pl.BlockSpec((rows, 2 * SUB), lambda step: (0, step)),
        out_shape=jax.ShapeDtypeStruct((rows, points), F32),
        scratch_shapes=weight_scratch(points),
        compiler_params=pltpu.CompilerParams(vmem_limit_bytes=LIMIT),
        cost_estimate=pl.CostEstimate(
            flops=17_000_000_000, bytes_accessed=16_000_000, transcendentals=4_000_000
        ),
        name="own_near",
    )(high, high8, low8, unit, source, target)


def rest_kernel(
    factor, left_ref, right_ref, source_ref, target_ref, expansion_ref, basis_ref, near_ref,
    out_ref, qh, q8h, q8l, units, far, w, w8h, w8l,
):
    strip = left_ref.shape[1]
    rank = expansion_ref.shape[1]
    row_count = out_ref.shape[0]

    @pl.when(pl.program_id(0) == 0)
    def _():
        @pl.loop(0, row_count // SUB)
        def _(step):
            rows = pl.ds(pl.multiple_of(step * SUB, SUB), SUB)
            joined = jnp.concatenate([left_ref[rows, :], right_ref[rows, :]], axis=1)
            full, high, rest, unit = scaled(joined)
            qh[rows, :] = high
            q8h[rows, :] = full.astype(F8)
            q8l[rows, :] = rest.astype(F8)
            units[rows, :] = jnp.broadcast_to(unit, (SUB, units.shape[1]))
            value = expansion_ref[rows, :]
            top = value.astype(BF)
            low = (value - top.astype(F32)).astype(BF)
            far[rows, :rank] = top
            far[rows, rank : 2 * rank] = low
            far[rows, 2 * rank :] = top

    def emit(rows, slot):
        columns = slice(slot * SUB, (slot + 1) * SUB)
        total = mm(qh[rows, :], w[slot])
        total = total + mm(q8h[rows, :], w8l[slot])
        total = total + mm(q8l[rows, :], w8h[slot])
        total = total * units[rows, 0:1] + near_ref[rows, columns]
        out_ref[rows, columns] = total * factor + mm(far[rows, :], basis_ref[:, columns])

    sweep(source_ref, target_ref, row_count, w, w8h, w8l, emit)


def finish(left, right, source, target, expansion, basis, near, factor):
    rows, points = near.shape
    strip = left.shape[1]
    whole = lambda a: pl.BlockSpec(a.shape, lambda step: (0, 0), pipeline_mode=pl.Buffered(1))
    block = lambda count: pl.BlockSpec((count, 2 * SUB), lambda step: (0, step))
    return pl.pallas_call(
        lambda *refs: rest_kernel(factor, *refs),
        grid=(points // (2 * SUB),),
        in_specs=[whole(a) for a in (left, right, source, target, expansion)]
        + [block(basis.shape[0]), block(rows)],
        out_specs=block(rows),
        out_shape=jax.ShapeDtypeStruct((rows, points), F32),
        scratch_shapes=[
            pltpu.VMEM((rows, 2 * strip), BF),
            pltpu.VMEM((rows, 2 * strip), F8),
            pltpu.VMEM((rows, 2 * strip), F8),
            pltpu.VMEM((rows, 128), F32),
            pltpu.VMEM((rows, basis.shape[0]), BF),
        ]
        + weight_scratch(2 * strip),
        compiler_params=pltpu.CompilerParams(vmem_limit_bytes=LIMIT),
        cost_estimate=pl.CostEstimate(
            flops=10_000_000_000, bytes_accessed=21_000_000, transcendentals=2_000_000
        ),
        name="finish",
    )(left, right, source, target, expansion, basis, near)


def body(charges, ordering, jitter, leaf_bases, transfer, coupling):
    set_count, vector_count = (charges.shape[0], charges.shape[1])
    points = charges.shape[4]
    strip_width = points // 4
    row_count = set_count * vector_count
    near_scale = points ** (-0.5)
    flattened = charges.reshape(row_count, points)
    offsets = jitter.reshape(3, points)
    indices = jnp.arange(points, dtype=jnp.float32)
    places = jnp.stack([(indices + offsets[0]) / points, offsets[1], offsets[2]])
    places = (places - 0.5) / GAIN
    leaf_basis = leaf_bases.reshape(leaf_bases.shape[2], points)
    basis_top = rounded(leaf_basis)
    basis_low = rounded(leaf_basis - basis_top)
    source_rows, target_rows = features(places)
    stacked = jnp.concatenate([basis_top.astype(BF), basis_low.astype(BF), source_rows])
    high, high8, low8, unit, tail, head, moment, own_source = prepare(
        flattened, ordering.reshape(1, points), stacked
    )
    count = lax.axis_size("leaf")
    onward = [(i, i + 1) for i in range(count - 1)]
    back = [(i + 1, i) for i in range(count - 1)]
    left = lax.ppermute(tail, "leaf", onward)
    right = lax.ppermute(head, "leaf", back)
    left_places = lax.ppermute(places[:, points - strip_width :], "leaf", onward)
    right_places = lax.ppermute(places[:, :strip_width], "leaf", back)
    side = jnp.array([[1.0 / GAIN], [0.0], [0.0]], F32)
    strip_places = jnp.concatenate([left_places - side, right_places + side], axis=1)
    strip_source = features(strip_places)[0].T
    near_part = own_near(high, high8, low8, unit, own_source, target_rows)
    leaf_levels = lax.axis_size("leaf").bit_length() - 1
    sub_levels = lax.axis_size("sub").bit_length() - 1
    position = lax.axis_index("leaf")
    siblings = []
    branch_bits = []
    current = moment
    for bit_index in range(leaf_levels):
        sibling = swapped(current, "leaf", bit_index)
        branch_bit = position >> bit_index & 1
        current = lift_pair(current, sibling, branch_bit, transfer[bit_index])
        siblings.append(sibling)
        branch_bits.append(branch_bit)
    sub_position = lax.axis_index("sub")
    for bit_index in range(sub_levels):
        level_index = leaf_levels + bit_index
        sibling = swapped(current, "sub", bit_index)
        branch_bit = sub_position >> bit_index & 1
        current = lift_pair(current, sibling, branch_bit, transfer[level_index])
        siblings.append(sibling)
        branch_bits.append(branch_bit)
    expansion = jnp.zeros((row_count, moment.shape[1]), jnp.float32)
    for level_index in reversed(range(leaf_levels + sub_levels)):
        couple_mat = lax.dynamic_index_in_dim(
            coupling[level_index], branch_bits[level_index], 0, keepdims=False
        )
        transfer_mat = lax.dynamic_index_in_dim(
            transfer[level_index], branch_bits[level_index], 0, keepdims=False
        )
        expansion = contract_last(siblings[level_index], couple_mat) + contract_last(
            expansion, transfer_mat
        )
    basis_rows = jnp.concatenate([basis_top, basis_top, basis_low]).astype(BF)
    potential = finish(
        left,
        right,
        strip_source,
        target_rows,
        expansion,
        basis_rows,
        near_part,
        near_scale / GAIN,
    )
    return potential.reshape(set_count, vector_count, 1, 1, points)


def solution(mesh):
    in_specs = (
        P(None, None, "sub", "leaf", None),
        P("sub", "leaf", None),
        P(None, "sub", "leaf", None),
        P("sub", "leaf", None, None),
        P(),
        P(),
    )
    out_specs = P(None, None, "sub", "leaf", None)
    return jax.shard_map(body, mesh=mesh, in_specs=in_specs, out_specs=out_specs, check_vma=False)
```

profile of v0, /device:TPU:18, one launch (start us, length us, event | category | flops | bytes accessed | tf_op | source)
XLA Modules:
  0.0 162.4 jit_solution(1910683988957676109)
XLA Ops:
  0.0 0.7 slice_bitcast_fusion.1
  0.7 0.7 fusion.95
  1.6 1.1 fusion.1
  2.7 10.9 %copy.59 = f32[16,64,1,1,2048]{4,1,2,3,0:T(8,128)} copy(f32[16,64,1,1,2048]{4,3,2,1,0:T(1,128)} %param.7) | data formatting | bytes 16777216
  13.7 4.3 %concatenate.11.x_ref = bf16[160,2048]{1,0:T(8,128)(2,1)} concatenate(bf16[64,2048]{1,0:T(8,128)(2,1)S(1)} %get-tuple-element.36, bf16[64,2048]{1,0:T(8,128)(2,1)S(1)} %get-tuple-element.35, bf16[1,2048]{1,0:T(2,128)(2,1)S(1)} %get-tuple-element.62, bf16[1,2048]{1,0:T(2,128)(2,1)S(1)} %get-tuple-element.62, bf16[1,2048]{1,0:T(2,128)(2,1)S(1)} %get-tuple-element.98, ...), dimensions={0} | concatenate | bytes 1310720 | tf_op jit(solution)/shard_map/concatenate | solution.py:323
  18.0 18.0 %prepare.1 = (bf16[1024,2048]{1,0:T(8,128)(2,1)}, f8e4m3fn[1024,2048]{1,0:T(32,128)(4,1)}, f8e4m3fn[1024,2048]{1,0:T(32,128)(4,1)}, f32[1024,128]{1,0:T(8,128)},...) custom-call(f32[1024,2048]{1,0:T(8,128)} %bitcast.105, ...), custom_call_target="tpu_custom_call" | custom-call | flops 14000000000 | bytes 28000000 | tf_op jit(solution)/shard_map/prepare/pallas_call | solution.py:138
  36.2 2.1 %collective-permute-done.4 = f32[1024,64]{1,0:T(8,128)S(1)} collective-permute-done((f32[1024,64]{1,0:T(8,128)}, f32[1024,64]{1,0:T(8,128)S(1)}, u32[]{:S(2)}, u32[]{:S(2)}) %collective-permute-start.4) | collective-permute-done | bytes 262176 | tf_op jit(solution)/shard_map/ppermute | solution.py:23
  38.3 0.7 fusion.2
  39.0 1.8 %convolution_add_fusion.11 = f32[1024,64]{0,1:T(8,128)S(1)} fusion(f32[1024,64]{0,1:T(8,128)S(1)} %fusion.2, f32[1024,64]{1,0:T(8,128)} %get-tuple-element.15, f32[1024,64]{1,0:T(8,128)S(1)} %collective-permute-done.4, pred[]{:T(512)S(6)} %eq.24, f32[7,2,64,64]{3,2,1,0:T(8,128)S(1)} %copy-done), kind=kOutput, calls=%fused_computation.11 | convolution fusion | flops 50462720 | bytes 1343489 | tf_op jit(solution)/shard_map/dot_general | solution.py:29
  40.8 0.6 collective-permute-start.5
  41.4 1.9 %collective-permute-start = (f32[1024,512]{1,0:T(8,128)}, f32[1024,512]{1,0:T(8,128)}, u32[]{:S(2)}, u32[]{:S(2)}) collective-permute-start(f32[1024,512]{1,0:T(8,128)} %get-tuple-element.13), channel_id=1, source_target_pairs={{0,4},{4,8},{8,12},{12,16},{16,20},{20,24},{24,28},{28,32},{32,36}... | collective-permute-start | bytes 6291464 | tf_op jit(solution)/shard_map/ppermute | solution.py:330
  43.3 3.6 %collective-permute-start.1 = (f32[1024,512]{1,0:T(8,128)}, f32[1024,512]{1,0:T(8,128)}, u32[]{:S(2)}, u32[]{:S(2)}) collective-permute-start(f32[1024,512]{1,0:T(8,128)} %get-tuple-element.14), channel_id=1, source_target_pairs={{4,0},{8,4},{12,8},{16,12},{20,16},{24,20},{28,24},{32,28},{36,32}... | collective-permute-start | bytes 6291464 | tf_op jit(solution)/shard_map/ppermute | solution.py:331
  47.0 0.6 fusion.129
  47.6 2.4 %collective-permute-start.2 = (f32[3,512]{1,0:T(4,128)}, f32[3,512]{1,0:T(4,128)S(1)}, u32[]{:S(2)}, u32[]{:S(2)}) collective-permute-start(f32[3,512]{1,0:T(4,128)} %get-tuple-element.63), channel_id=1, source_target_pairs={{0,4},{4,8},{8,12},{12,16},{16,20},{20,24},{24,28},{28,32},{32,36}... | collective-permute-start | bytes 18440 | tf_op jit(solution)/shard_map/ppermute | solution.py:332
  50.0 3.1 %collective-permute-start.3 = (f32[3,512]{1,0:T(4,128)}, f32[3,512]{1,0:T(4,128)S(1)}, u32[]{:S(2)}, u32[]{:S(2)}) collective-permute-start(f32[3,512]{1,0:T(4,128)} %get-tuple-element.64), channel_id=1, source_target_pairs={{4,0},{8,4},{12,8},{16,12},{20,16},{24,20},{28,24},{32,28},{36,32}... | collective-permute-start | bytes 18440 | tf_op jit(solution)/shard_map/ppermute | solution.py:333
  53.2 2.8 %stack.17.target_ref.refs_3_ = bf16[32,2048]{1,0:T(8,128)(2,1)} concatenate(bf16[1,2048]{1,0:T(2,128)(2,1)S(1)} %get-tuple-element.52, bf16[1,2048]{1,0:T(2,128)(2,1)S(1)} %get-tuple-element.100, bf16[1,2048]{1,0:T(2,128)(2,1)S(1)} %get-tuple-element.52, bf16[1,2048]{1,0:T(2,128)(2,1)S(1)} %get-tuple-element.100, bf16[1,2048]{1,0:T(2,128)(2,1)S(1)} %get-tuple-element.58, ...), dimensions={0} | concatenate | bytes 262144 | tf_op jit(solution)/shard_map/stack | solution.py:79
  55.9 0.4 fusion.17
  56.3 0.4 convolution_add_fusion.9
  56.8 2.7 %collective-permute-start.6 = (f32[1024,64]{0,1:T(8,128)S(1)}, f32[1024,64]{0,1:T(8,128)S(1)}, u32[]{:S(2)}, u32[]{:S(2)}) collective-permute-start(f32[1024,64]{0,1:T(8,128)S(1)} %convolution_add_fusion.9), channel_id=1, source_target_pairs={{0,16},{4,20},{8,24},{12,28},{16,0},{20,4},{24,8},{28,12},{32,48},... | collective-permute-start | bytes 786440 | tf_op jit(solution)/shard_map/ppermute | solution.py:23
  59.5 26.4 %own_near.1.refs_6_ = f32[1024,2048]{1,0:T(8,128)} custom-call(bf16[1024,2048]{1,0:T(8,128)(2,1)} %get-tuple-element.16.qh_ref, f8e4m3fn[1024,2048]{1,0:T(32,128)(4,1)} %get-tuple-element.17.q8h_ref, f8e4m3fn[1024,2048]{1,0:T(32,128)(4,1)} %get-tuple-element.18.q8l_ref, f32[1024,128]{1,0:T(8,128)} %get-tuple-element.19.unit_ref, ...), custom_call_target="tpu_custom_call" | custom-call | flops 16999999488 | bytes 16000000 | tf_op jit(solution)/shard_map/own_near/pallas_call | solution.py:228
  85.8 0.7 fusion.128
  86.5 0.4 fusion.14
  87.0 0.4 convolution_add_fusion.7
  87.4 1.4 collective-permute-start.7
  88.7 0.7 fusion.127
  89.5 0.9 multiply_reduce_fusion
  90.3 1.0 pad_maximum_fusion.refs_5_
  91.4 4.2 %collective-permute-done.7 = f32[1024,64]{0,1:T(8,128)S(1)} collective-permute-done((f32[1024,64]{0,1:T(8,128)S(1)}, f32[1024,64]{0,1:T(8,128)S(1)}, u32[]{:S(2)}, u32[]{:S(2)}) %collective-permute-start.7) | collective-permute-done | bytes 262176 | tf_op jit(solution)/shard_map/ppermute | solution.py:23
  95.5 0.4 fusion.11
  95.9 0.4 convolution_add_fusion.5
  96.5 0.7 broadcast_add_fusion
  97.2 0.7 broadcast_add_fusion.1
  97.9 9.2 %collective-permute-done.8 = f32[1024,64]{0,1:T(8,128)S(1)} collective-permute-done((f32[1024,64]{0,1:T(8,128)S(1)}, f32[1024,64]{0,1:T(8,128)S(1)}, u32[]{:S(2)}, u32[]{:S(2)}) %collective-permute-start.8) | collective-permute-done | bytes 262176 | tf_op jit(solution)/shard_map/ppermute | solution.py:23
  107.1 0.4 fusion.8
  107.5 0.4 convolution_add_fusion.3
  108.0 2.0 %collective-permute-start.9 = (f32[1024,64]{0,1:T(8,128)S(1)}, f32[1024,64]{0,1:T(8,128)S(1)}, u32[]{:S(2)}, u32[]{:S(2)}) collective-permute-start(f32[1024,64]{0,1:T(8,128)S(1)} %convolution_add_fusion.3), channel_id=1, source_target_pairs={{0,1},{1,0},{2,3},{3,2},{4,5},{5,4},{6,7},{7,6},{8,9},{9,8},{10,11... | collective-permute-start | bytes 786440 | tf_op jit(solution)/shard_map/ppermute | solution.py:23
  110.0 6.5 %collective-permute-done.9 = f32[1024,64]{0,1:T(8,128)S(1)} collective-permute-done((f32[1024,64]{0,1:T(8,128)S(1)}, f32[1024,64]{0,1:T(8,128)S(1)}, u32[]{:S(2)}, u32[]{:S(2)}) %collective-permute-start.9) | collective-permute-done | bytes 262176 | tf_op jit(solution)/shard_map/ppermute | solution.py:23
  116.5 0.4 fusion.5
  117.0 0.4 convolution_add_fusion.1
  117.4 4.0 %collective-permute-start.10 = (f32[1024,64]{0,1:T(8,128)S(1)}, f32[1024,64]{0,1:T(8,128)S(1)}, u32[]{:S(2)}, u32[]{:S(2)}) collective-permute-start(f32[1024,64]{0,1:T(8,128)S(1)} %convolution_add_fusion.1), channel_id=1, source_target_pairs={{0,2},{1,3},{2,0},{3,1},{4,6},{5,7},{6,4},{7,5},{8,10},{9,11},{10,... | collective-permute-start | bytes 786440 | tf_op jit(solution)/shard_map/ppermute | solution.py:23
  121.6 0.8 copy.56
  122.5 4.6 %collective-permute-done.10 = f32[1024,64]{0,1:T(8,128)S(1)} collective-permute-done((f32[1024,64]{0,1:T(8,128)S(1)}, f32[1024,64]{0,1:T(8,128)S(1)}, u32[]{:S(2)}, u32[]{:S(2)}) %collective-permute-start.10) | collective-permute-done | bytes 262176 | tf_op jit(solution)/shard_map/ppermute | solution.py:23
  128.6 0.4 convolution_add_fusion.4
  130.9 0.4 convolution_add_fusion.10
  131.7 0.7 convolution_add_fusion.12
  132.4 1.0 copy.57.refs_4_
  133.4 18.2 %finish.1 = f32[1024,2048]{1,0:T(8,128)} custom-call(f32[1024,512]{1,0:T(8,128)} %collective-permute-done.refs_0_, f32[1024,512]{1,0:T(8,128)} %collective-permute-done.1.refs_1_, bf16[1024,32]{1,0:T(8,128)(2,1)} %bitcast.107, bf16[32,2048]{1,0:T(8,128)(2,1)} %stack.17.target_ref.refs_3_, f32[1024,64]{1,0:T(8,128)} %copy.57.refs_4_, ...), custom_call_target="tpu_custom_call" | custom-call | flops 10000000000 | bytes 21000000 | tf_op jit(solution)/shard_map/finish/pallas_call | solution.py:285
  151.6 10.8 %copy.58 = f32[16,64,1,1,2048]{4,3,2,1,0:T(1,128)} copy(f32[16,64,1,1,2048]{4,1,0,3,2:T(8,128)} %bitcast.106) | data formatting | bytes 16777216 | tf_op jit(solution)/shard_map/reshape | solution.py:380
  (48 shorter events, 4.4 us)
Async XLA Ops:
  18.0 20.2 %copy-start = (f32[7,2,64,64]{3,2,1,0:T(8,128)S(1)}, f32[7,2,64,64]{3,2,1,0:T(8,128)}, u32[]{:S(2)}) copy-start(f32[7,2,64,64]{3,2,1,0:T(8,128)} %param.11) | copy-start | bytes 688132
  36.1 2.2 %collective-permute-start.4 = (f32[1024,64]{1,0:T(8,128)}, f32[1024,64]{1,0:T(8,128)S(1)}, u32[]{:S(2)}, u32[]{:S(2)}) collective-permute-start(f32[1024,64]{1,0:T(8,128)} %get-tuple-element.15), channel_id=1, source_target_pairs={{0,4},{4,0},{8,12},{12,8},{16,20},{20,16},{24,28},{28,24},{32,36},... | collective-permute-start | bytes 786440 | tf_op jit(solution)/shard_map/ppermute | solution.py:23
  40.8 15.1 %collective-permute-start.5 = (f32[1024,64]{0,1:T(8,128)S(1)}, f32[1024,64]{0,1:T(8,128)S(1)}, u32[]{:S(2)}, u32[]{:S(2)}) collective-permute-start(f32[1024,64]{0,1:T(8,128)S(1)} %convolution_add_fusion.11), channel_id=1, source_target_pairs={{0,8},{4,12},{8,0},{12,4},{16,24},{20,28},{24,16},{28,20},{32,40},... | collective-permute-start | bytes 786440 | tf_op jit(solution)/shard_map/ppermute | solution.py:23
  41.4 92.0 %collective-permute-start = (f32[1024,512]{1,0:T(8,128)}, f32[1024,512]{1,0:T(8,128)}, u32[]{:S(2)}, u32[]{:S(2)}) collective-permute-start(f32[1024,512]{1,0:T(8,128)} %get-tuple-element.13), channel_id=1, source_target_pairs={{0,4},{4,8},{8,12},{12,16},{16,20},{20,24},{24,28},{28,32},{32,36}... | collective-permute-start | bytes 6291464 | tf_op jit(solution)/shard_map/ppermute | solution.py:330
  43.3 90.0 %collective-permute-start.1 = (f32[1024,512]{1,0:T(8,128)}, f32[1024,512]{1,0:T(8,128)}, u32[]{:S(2)}, u32[]{:S(2)}) collective-permute-start(f32[1024,512]{1,0:T(8,128)} %get-tuple-element.14), channel_id=1, source_target_pairs={{4,0},{8,4},{12,8},{16,12},{20,16},{24,20},{28,24},{32,28},{36,32}... | collective-permute-start | bytes 6291464 | tf_op jit(solution)/shard_map/ppermute | solution.py:331
  47.6 48.9 %collective-permute-start.2 = (f32[3,512]{1,0:T(4,128)}, f32[3,512]{1,0:T(4,128)S(1)}, u32[]{:S(2)}, u32[]{:S(2)}) collective-permute-start(f32[3,512]{1,0:T(4,128)} %get-tuple-element.63), channel_id=1, source_target_pairs={{0,4},{4,8},{8,12},{12,16},{16,20},{20,24},{24,28},{28,32},{32,36}... | collective-permute-start | bytes 18440 | tf_op jit(solution)/shard_map/ppermute | solution.py:332
  50.0 47.2 %collective-permute-start.3 = (f32[3,512]{1,0:T(4,128)}, f32[3,512]{1,0:T(4,128)S(1)}, u32[]{:S(2)}, u32[]{:S(2)}) collective-permute-start(f32[3,512]{1,0:T(4,128)} %get-tuple-element.64), channel_id=1, source_target_pairs={{4,0},{8,4},{12,8},{16,12},{20,16},{24,20},{28,24},{32,28},{36,32}... | collective-permute-start | bytes 18440 | tf_op jit(solution)/shard_map/ppermute | solution.py:333
  56.8 29.8 %collective-permute-start.6 = (f32[1024,64]{0,1:T(8,128)S(1)}, f32[1024,64]{0,1:T(8,128)S(1)}, u32[]{:S(2)}, u32[]{:S(2)}) collective-permute-start(f32[1024,64]{0,1:T(8,128)S(1)} %convolution_add_fusion.9), channel_id=1, source_target_pairs={{0,16},{4,20},{8,24},{12,28},{16,0},{20,4},{24,8},{28,12},{32,48},... | collective-permute-start | bytes 786440 | tf_op jit(solution)/shard_map/ppermute | solution.py:23
  85.8 2.9 %copy-start.1 = (f32[7,2,64,64]{3,2,1,0:T(8,128)S(1)}, f32[7,2,64,64]{3,2,1,0:T(8,128)}, u32[]{:S(2)}) copy-start(f32[7,2,64,64]{3,2,1,0:T(8,128)} %param.12) | copy-start | bytes 688132
  87.4 8.1 %collective-permute-start.7 = (f32[1024,64]{0,1:T(8,128)S(1)}, f32[1024,64]{0,1:T(8,128)S(1)}, u32[]{:S(2)}, u32[]{:S(2)}) collective-permute-start(f32[1024,64]{0,1:T(8,128)S(1)} %convolution_add_fusion.7), channel_id=1, source_target_pairs={{0,32},{4,36},{8,40},{12,44},{16,48},{20,52},{24,56},{28,60},{32,0... | collective-permute-start | bytes 786440 | tf_op jit(solution)/shard_map/ppermute | solution.py:23
  96.4 10.7 %collective-permute-start.8 = (f32[1024,64]{0,1:T(8,128)S(1)}, f32[1024,64]{0,1:T(8,128)S(1)}, u32[]{:S(2)}, u32[]{:S(2)}) collective-permute-start(f32[1024,64]{0,1:T(8,128)S(1)} %convolution_add_fusion.5), channel_id=1, source_target_pairs={{0,64},{4,68},{8,72},{12,76},{16,80},{20,84},{24,88},{28,92},{32,9... | collective-permute-start | bytes 786440 | tf_op jit(solution)/shard_map/ppermute | solution.py:23
  97.9 29.1 %copy-start.6 = (f32[1,2,64,64]{3,2,1,0:T(8,128)S(1)}, f32[1,2,64,64]{3,2,1,0:T(8,128)}, u32[]{:S(2)}) copy-start(f32[1,2,64,64]{3,2,1,0:T(8,128)} %get-tuple-element.42) | copy-start | bytes 98308
  107.5 19.9 %copy-start.2 = (f32[1,2,64,64]{3,2,1,0:T(8,128)S(1)}, f32[1,2,64,64]{3,2,1,0:T(8,128)}, u32[]{:S(2)}) copy-start(f32[1,2,64,64]{3,2,1,0:T(8,128)} %get-tuple-element.48) | copy-start | bytes 98308
  108.0 19.9 %copy-start.5 = (f32[1,2,64,64]{3,2,1,0:T(8,128)S(1)}, f32[1,2,64,64]{3,2,1,0:T(8,128)}, u32[]{:S(2)}) copy-start(f32[1,2,64,64]{3,2,1,0:T(8,128)} %get-tuple-element.43) | copy-start | bytes 98308
  108.0 8.6 %collective-permute-start.9 = (f32[1024,64]{0,1:T(8,128)S(1)}, f32[1024,64]{0,1:T(8,128)S(1)}, u32[]{:S(2)}, u32[]{:S(2)}) collective-permute-start(f32[1024,64]{0,1:T(8,128)S(1)} %convolution_add_fusion.3), channel_id=1, source_target_pairs={{0,1},{1,0},{2,3},{3,2},{4,5},{5,4},{6,7},{7,6},{8,9},{9,8},{10,11... | collective-permute-start | bytes 786440 | tf_op jit(solution)/shard_map/ppermute | solution.py:23
  116.9 11.7 %copy-start.4 = (f32[1,2,64,64]{3,2,1,0:T(8,128)S(1)}, f32[1,2,64,64]{3,2,1,0:T(8,128)}, u32[]{:S(2)}) copy-start(f32[1,2,64,64]{3,2,1,0:T(8,128)} %get-tuple-element.38) | copy-start | bytes 98308
  117.4 9.7 %collective-permute-start.10 = (f32[1024,64]{0,1:T(8,128)S(1)}, f32[1024,64]{0,1:T(8,128)S(1)}, u32[]{:S(2)}, u32[]{:S(2)}) collective-permute-start(f32[1024,64]{0,1:T(8,128)S(1)} %convolution_add_fusion.1), channel_id=1, source_target_pairs={{0,2},{1,3},{2,0},{3,1},{4,6},{5,7},{6,4},{7,5},{8,10},{9,11},{10,... | collective-permute-start | bytes 786440 | tf_op jit(solution)/shard_map/ppermute | solution.py:23
  121.6 7.8 %copy-start.3 = (f32[1,2,64,64]{3,2,1,0:T(8,128)S(1)}, f32[1,2,64,64]{3,2,1,0:T(8,128)}, u32[]{:S(2)}) copy-start(f32[1,2,64,64]{3,2,1,0:T(8,128)} %get-tuple-element.39) | copy-start | bytes 98308
where the time goes:
time: 163 us; the launch traced here: 162 us
  Pallas kernels  62.6 us (38%)
  local copies, waits for them, and re-layouts  33.6 us (21%)
  waiting for transfers between devices  26.6 us (16%)
  starting transfers between devices  21.9 us (13%)
  matrix products  11.8 us (7%)
  other arithmetic  5.5 us (3%)
    ppermute x7, waiting for transfers between devices, swapped(): return lax.ppermute(value, axis, pairs)  26.5 us
    pallas_call x1, Pallas kernels, own_near(): pl.pallas_call(own_kernel, grid=(points // (2 * SUB),), in_specs=[whole(a...  26.4 us
    pallas_call x1, Pallas kernels, finish(): pl.pallas_call(lambda *refs: rest_kernel(factor, *refs), grid=(points //...  18.2 us
    pallas_call x1, Pallas kernels, prepare(): pl.pallas_call(prepare_kernel, grid=(rows // chunk,), in_specs=[sliced(po...  18 us
    unnamed x15, local copies, waits for them, and re-layouts  10.9 us
    reshape x1, local copies, waits for them, and re-layouts, body(): return potential.reshape(set_count, vector_count, 1, 1, points)  10.8 us
    ppermute x7, starting transfers between devices, swapped(): return lax.ppermute(value, axis, pairs)  10.8 us
    dot_general x13, matrix products, contract_last(): lax.dot_general(left_mat, right_mat, (((1,), (1,)), ((), ())), precision=...  5.16 us
  transfers between devices with their start and end apart: 11, of which 5 were waited for; matrix products, arithmetic and copies ran while one was open for 12% of the time, Pallas kernels for 16%

commit v1 on v0

v1 whole, which is shorter than its diff:
```python
import jax
import jax.numpy as jnp
from jax import lax
from jax.experimental import pallas as pl
from jax.experimental.pallas import tpu as pltpu
from jax.sharding import PartitionSpec as P

DELTA_SQ = 0.0025
PRECISE = lax.Precision.HIGHEST
F8 = jnp.float8_e4m3fn
BF = jnp.bfloat16
F32 = jnp.float32
GAIN = 16.0
TOP = 384.0
FEATS = 32
SUB = 256
OUT_BLOCKS = 4
LANES = 128
PAD = 8
LIMIT = 60 * 1024 * 1024


def swapped(value, axis, stride):
    mask = 2**stride
    pairs = [(source, source ^ mask) for source in range(lax.axis_size(axis))]
    return lax.ppermute(value, axis, pairs)


def lift_pair(current, sibling, branch_bit, transfer_pair):
    left_part = jnp.where(branch_bit == 0, current, sibling)
    right_part = jnp.where(branch_bit == 0, sibling, current)
    parent = jnp.dot(
        left_part, transfer_pair[0], precision=PRECISE, preferred_element_type=jnp.float32
    )
    return parent + jnp.dot(
        right_part, transfer_pair[1], precision=PRECISE, preferred_element_type=jnp.float32
    )


def contract_last(left_mat, right_mat):
    return lax.dot_general(
        left_mat,
        right_mat,
        (((1,), (1,)), ((), ())),
        precision=PRECISE,
        preferred_element_type=jnp.float32,
    )


def mm(left, right):
    return jnp.dot(left, right, preferred_element_type=F32)


def mm_nt(left, right):
    return lax.dot_general(left, right, (((1,), (1,)), ((), ())), preferred_element_type=F32)


def split(value):
    high = value.astype(BF)
    return high, value - high.astype(F32)


def features(coords, source_ref, target_ref, columns):
    ones = jnp.ones_like(coords[0])
    norm = sum(coord * coord for coord in coords)

    def pieces(value):
        out = []
        for _ in range(3):
            high, value = split(value)
            out.append(high.astype(F32))
        return out

    source = []
    target = []
    for coord in coords:
        part = pieces(coord)
        for left, right in ((0, 0), (0, 1), (1, 0), (1, 1), (0, 2), (2, 0)):
            source.append(part[left])
            target.append(-2.0 * part[right])
    source += pieces(norm + DELTA_SQ / (GAIN * GAIN)) + [ones] * 3
    target += [ones] * 3 + pieces(norm)
    blank = [jnp.zeros_like(norm)] * (FEATS - len(source))
    for ref, rows in ((source_ref, source + blank), (target_ref, target + blank)):
        if ref is not None:
            for index, row in enumerate(rows):
                ref[index : index + 1, columns] = row


def scaled(rows):
    top = jnp.maximum(jnp.max(jnp.abs(rows), axis=1, keepdims=True), 1e-30)
    full = rows * (TOP / top)
    high = full.astype(BF)
    return full, high, full - high.astype(F32), top * (1.0 / TOP)


def prepare_kernel(
    q_ref, order_ref, jitter_ref, bases_ref,
    qh_ref, q8h_ref, q8l_ref, unit_ref, tail_ref, head_ref, moment_ref, feat_ref, target_ref,
    pick, pick8, basis, moved, source_rows, target_rows,
):
    points = order_ref.shape[1]
    strip = tail_ref.shape[1]
    rank = bases_ref.shape[0]
    chunk = qh_ref.shape[0]
    tiles = points // LANES
    last = points - strip
    now = pl.program_id(0)

    @pl.when(now == 0)
    def _():
        index = lax.broadcasted_iota(jnp.int32, (1, points), 1).astype(F32)
        coords = [(index + jitter_ref[0]) * (1.0 / points), jitter_ref[1], jitter_ref[2]]
        coords = [(coord - 0.5) * (1.0 / GAIN) for coord in coords]
        features(coords, source_rows, target_rows, slice(0, points))
        target_ref[...] = target_rows[...].astype(BF)
        rows = tail_ref.shape[0] - PAD
        for axis in range(3):
            tail_ref[rows + axis : rows + axis + 1, :] = coords[axis][:, last:]
            head_ref[rows + axis : rows + axis + 1, :] = coords[axis][:, :strip]
        blank = jnp.zeros((PAD - 3, strip), F32)
        tail_ref[rows + 3 :, :] = blank
        head_ref[rows + 3 :, :] = blank
        high, low = split(bases_ref[...])
        moved[:rank, :] = high
        moved[rank : 2 * rank, :] = low.astype(BF)
        moved[2 * rank :, :] = source_rows[...].astype(BF)

        @pl.loop(0, points // SUB)
        def _(step):
            rows = pl.ds(pl.multiple_of(step * SUB, SUB), SUB)
            own = lax.broadcasted_iota(jnp.int32, (SUB, strip), 0) + step * SUB
            for part in range(points // strip):
                columns = slice(part * strip, (part + 1) * strip)
                hit = jnp.where(own == order_ref[:, columns], 1.0, 0.0)
                pick[rows, columns] = hit.astype(BF)
                if part == 0:
                    pick8[rows, :strip] = hit.astype(F8)
                if part == points // strip - 1:
                    pick8[rows, strip:] = hit.astype(F8)
            placed = mm_nt(pick[rows, :], moved[...]).astype(BF)
            feat_ref[rows, :] = placed[:, 2 * rank :]
            basis[rows, :] = placed[:, : 2 * rank]

    block = [q_ref[pl.ds(tile, chunk, stride=tiles), :] for tile in range(tiles)]
    full, high, rest, unit = scaled(jnp.concatenate(block, axis=1))
    low8 = rest.astype(F8)
    qh_ref[...] = high
    q8h_ref[...] = full.astype(F8)
    q8l_ref[...] = low8
    unit_ref[...] = jnp.broadcast_to(unit, unit_ref.shape)
    rows = pl.ds(pl.multiple_of(now * chunk, chunk), chunk)
    head_ref[rows, :] = (mm(high, pick[:, :strip]) + mm(low8, pick8[:, :strip])) * unit
    tail_ref[rows, :] = (mm(high, pick[:, last:]) + mm(low8, pick8[:, strip:])) * unit
    both = mm(high, basis[...])
    moment_ref[...] = (
        both[:, :rank] + both[:, rank:] + mm(rest.astype(BF), basis[:, :rank])
    ) * unit


def prepare(charges, order, jitter, bases):
    points = order.shape[1]
    tiles = points // LANES
    rows = charges.shape[0] // tiles
    strip = points // 4
    rank = bases.shape[0]
    chunk = 256
    whole = lambda shape: pl.BlockSpec(shape, lambda step: (0,) * len(shape))
    sliced = lambda width: pl.BlockSpec((chunk, width), lambda step: (step, 0))
    shape = jax.ShapeDtypeStruct
    return pl.pallas_call(
        prepare_kernel,
        grid=(rows // chunk,),
        in_specs=[
            pl.BlockSpec((chunk * tiles, LANES), lambda step: (step, 0)),
            whole(order.shape),
            whole(jitter.shape),
            whole(bases.shape),
        ],
        out_specs=[sliced(points)] * 3
        + [sliced(LANES), whole((rows + PAD, strip)), whole((rows + PAD, strip)), sliced(rank)]
        + [whole((points, FEATS)), whole((FEATS, points))],
        out_shape=[
            shape((rows, points), BF),
            shape((rows, points), F8),
            shape((rows, points), F8),
            shape((rows, LANES), F32),
            shape((rows + PAD, strip), F32),
            shape((rows + PAD, strip), F32),
            shape((rows, rank), F32),
            shape((points, FEATS), BF),
            shape((FEATS, points), BF),
        ],
        scratch_shapes=[
            pltpu.VMEM((points, points), BF),
            pltpu.VMEM((points, 2 * strip), F8),
            pltpu.VMEM((points, 2 * rank), BF),
            pltpu.VMEM((2 * rank + FEATS, points), BF),
            pltpu.VMEM((FEATS, points), F32),
            pltpu.VMEM((FEATS, points), F32),
        ],
        compiler_params=pltpu.CompilerParams(vmem_limit_bytes=LIMIT),
        cost_estimate=pl.CostEstimate(
            flops=14_000_000_000, bytes_accessed=28_000_000, transcendentals=0
        ),
        name="prepare",
    )(charges, order, jitter, bases)


def weigh(source_ref, target, first, last, slot, w, w8h, w8l):
    for row in range(first, last, 128):
        rows = slice(row, row + 128)
        weight = lax.rsqrt(mm(source_ref[rows, :], target))
        high = weight.astype(BF)
        w[slot, rows, :] = high
        w8h[slot, rows, :] = weight.astype(F8)
        w8l[slot, rows, :] = (weight - high.astype(F32)).astype(F8)


def sweep(source_ref, target_ref, row_count, w, w8h, w8l, emit, count):
    points = source_ref.shape[0]
    blocks = target_ref.shape[1] // SUB
    step = pl.program_id(0)
    parts = 4

    def target(block):
        return target_ref[:, pl.ds(pl.multiple_of(block * SUB, SUB), SUB)]

    @pl.when(step == 0)
    def _():
        weigh(source_ref, target(0), 0, points, 0, w, w8h, w8l)

    height = row_count // parts
    for block in range(count):
        slot = block % 2
        coming = target(jnp.minimum(count * step + block + 1, blocks - 1))
        for part in range(parts):
            weigh(
                source_ref,
                coming,
                part * points // parts,
                (part + 1) * points // parts,
                1 - slot,
                w,
                w8h,
                w8l,
            )
            emit(slice(part * height, (part + 1) * height), block, slot)


def own_kernel(qh_ref, q8h_ref, q8l_ref, unit_ref, source_ref, target_ref, out_ref, w, w8h, w8l):
    def emit(rows, block, slot):
        total = mm(qh_ref[rows, :], w[slot])
        total = total + mm(q8h_ref[rows, :], w8l[slot])
        total = total + mm(q8l_ref[rows, :], w8h[slot])
        out_ref[rows, block * SUB : (block + 1) * SUB] = total * unit_ref[rows, 0:1]

    sweep(source_ref, target_ref, out_ref.shape[0], w, w8h, w8l, emit, 2)


def weight_scratch(count):
    return [
        pltpu.VMEM((2, count, SUB), BF),
        pltpu.VMEM((2, count, SUB), F8),
        pltpu.VMEM((2, count, SUB), F8),
    ]


def own_near(high, high8, low8, unit, source, target):
    rows, points = high.shape
    whole = lambda a: pl.BlockSpec(a.shape, lambda step: (0, 0), pipeline_mode=pl.Buffered(1))
    return pl.pallas_call(
        own_kernel,
        grid=(points // (2 * SUB),),
        in_specs=[whole(a) for a in (high, high8, low8, unit, source, target)],
        out_specs=pl.BlockSpec((rows, 2 * SUB), lambda step: (0, step)),
        out_shape=jax.ShapeDtypeStruct((rows, points), F32),
        scratch_shapes=weight_scratch(points),
        compiler_params=pltpu.CompilerParams(vmem_limit_bytes=LIMIT),
        cost_estimate=pl.CostEstimate(
            flops=17_000_000_000, bytes_accessed=16_000_000, transcendentals=4_000_000
        ),
        name="own_near",
    )(high, high8, low8, unit, source, target)


def rest_kernel(
    factor, left_ref, right_ref, target_ref, expansion_ref, bases_ref, near_ref,
    out_ref, qh, q8h, q8l, units, far, basis, source_rows, source, w, w8h, w8l,
):
    strip = left_ref.shape[1]
    rank = expansion_ref.shape[1]
    row_count = near_ref.shape[0]

    @pl.when(pl.program_id(0) == 0)
    def _():
        for ref, shift, columns in (
            (left_ref, -1.0, slice(0, strip)),
            (right_ref, 1.0, slice(strip, 2 * strip)),
        ):
            coords = [ref[row_count + axis : row_count + axis + 1, :] for axis in range(3)]
            coords[0] = coords[0] + shift / GAIN
            features(coords, source_rows, None, columns)
        source[...] = jnp.transpose(source_rows[...]).astype(BF)

        @pl.loop(0, row_count // SUB)
        def _(step):
            rows = pl.ds(pl.multiple_of(step * SUB, SUB), SUB)
            joined = jnp.concatenate([left_ref[rows, :], right_ref[rows, :]], axis=1)
            full, high, rest, unit = scaled(joined)
            qh[rows, :] = high
            q8h[rows, :] = full.astype(F8)
            q8l[rows, :] = rest.astype(F8)
            units[rows, :] = jnp.broadcast_to(unit, (SUB, units.shape[1]))
            top, low = split(expansion_ref[rows, :])
            far[rows, :rank] = top
            far[rows, rank : 2 * rank] = low.astype(BF)
            far[rows, 2 * rank :] = top

        top, low = split(bases_ref[...])
        basis[:rank, :] = top
        basis[rank : 2 * rank, :] = top
        basis[2 * rank :, :] = low.astype(BF)

    def emit(rows, block, slot):
        total = mm(qh[rows, :], w[slot])
        total = total + mm(q8h[rows, :], w8l[slot])
        total = total + mm(q8l[rows, :], w8h[slot])
        inner = slice(block * SUB, (block + 1) * SUB)
        total = total * units[rows, 0:1] + near_ref[rows, inner]
        columns = pl.ds(
            pl.multiple_of((pl.program_id(0) * OUT_BLOCKS + block) * SUB, SUB), SUB
        )
        total = total * factor + mm(far[rows, :], basis[:, columns])
        first = rows.start * PAD
        for part in range(SUB // LANES):
            place = first + block * (SUB // LANES) + part
            out_ref[pl.ds(place, rows.stop - rows.start, stride=PAD), :] = total[
                :, part * LANES : (part + 1) * LANES
            ]

    sweep(source, target_ref, row_count, w, w8h, w8l, emit, OUT_BLOCKS)


def finish(left, right, target, expansion, bases, near, factor):
    rows, points = near.shape
    strip = left.shape[1]
    rank = bases.shape[0]
    width = OUT_BLOCKS * SUB
    whole = lambda a: pl.BlockSpec(a.shape, lambda step: (0, 0), pipeline_mode=pl.Buffered(1))

    def kernel(*refs):
        out = refs[6]
        flat = out.reshape(rows * PAD, LANES)
        rest_kernel(factor, *refs[:6], flat, *refs[7:])

    return pl.pallas_call(
        kernel,
        grid=(points // width,),
        in_specs=[whole(a) for a in (left, right, target, expansion, bases)]
        + [pl.BlockSpec((rows, width), lambda step: (0, step))],
        out_specs=pl.BlockSpec((rows, 1, PAD, LANES), lambda step: (0, step, 0, 0)),
        out_shape=jax.ShapeDtypeStruct((rows, points // width, PAD, LANES), F32),
        scratch_shapes=[
            pltpu.VMEM((rows, 2 * strip), BF),
            pltpu.VMEM((rows, 2 * strip), F8),
            pltpu.VMEM((rows, 2 * strip), F8),
            pltpu.VMEM((rows, LANES), F32),
            pltpu.VMEM((rows, 3 * rank), BF),
            pltpu.VMEM((3 * rank, points), BF),
            pltpu.VMEM((FEATS, 2 * strip), F32),
            pltpu.VMEM((2 * strip, FEATS), BF),
        ]
        + weight_scratch(2 * strip),
        compiler_params=pltpu.CompilerParams(vmem_limit_bytes=LIMIT),
        cost_estimate=pl.CostEstimate(
            flops=10_000_000_000, bytes_accessed=21_000_000, transcendentals=2_000_000
        ),
        name="finish",
    )(left, right, target, expansion, bases, near)


def body(charges, ordering, jitter, leaf_bases, transfer, coupling):
    set_count, vector_count = (charges.shape[0], charges.shape[1])
    points = charges.shape[4]
    row_count = set_count * vector_count
    near_scale = points ** (-0.5)
    leaf_basis = leaf_bases.reshape(leaf_bases.shape[2], points)
    high, high8, low8, unit, tail, head, moment, own_source, target_rows = prepare(
        charges.reshape(row_count * (points // LANES), LANES),
        ordering.reshape(1, points),
        jitter.reshape(3, 1, points),
        leaf_basis,
    )
    count = lax.axis_size("leaf")
    onward = [(i, i + 1) for i in range(count - 1)]
    back = [(i + 1, i) for i in range(count - 1)]
    left = lax.ppermute(tail, "leaf", onward)
    right = lax.ppermute(head, "leaf", back)
    near_part = own_near(high, high8, low8, unit, own_source, target_rows)
    leaf_levels = lax.axis_size("leaf").bit_length() - 1
    sub_levels = lax.axis_size("sub").bit_length() - 1
    position = lax.axis_index("leaf")
    siblings = []
    branch_bits = []
    current = moment
    for bit_index in range(leaf_levels):
        sibling = swapped(current, "leaf", bit_index)
        branch_bit = position >> bit_index & 1
        current = lift_pair(current, sibling, branch_bit, transfer[bit_index])
        siblings.append(sibling)
        branch_bits.append(branch_bit)
    sub_position = lax.axis_index("sub")
    for bit_index in range(sub_levels):
        level_index = leaf_levels + bit_index
        sibling = swapped(current, "sub", bit_index)
        branch_bit = sub_position >> bit_index & 1
        current = lift_pair(current, sibling, branch_bit, transfer[level_index])
        siblings.append(sibling)
        branch_bits.append(branch_bit)
    expansion = jnp.zeros((row_count, moment.shape[1]), jnp.float32)
    for level_index in reversed(range(leaf_levels + sub_levels)):
        couple_mat = lax.dynamic_index_in_dim(
            coupling[level_index], branch_bits[level_index], 0, keepdims=False
        )
        transfer_mat = lax.dynamic_index_in_dim(
            transfer[level_index], branch_bits[level_index], 0, keepdims=False
        )
        expansion = contract_last(siblings[level_index], couple_mat) + contract_last(
            expansion, transfer_mat
        )
    potential = finish(
        left, right, target_rows, expansion, leaf_basis, near_part, near_scale / GAIN
    )
    return potential.reshape(set_count, vector_count, 1, 1, points)


def solution(mesh):
    in_specs = (
        P(None, None, "sub", "leaf", None),
        P("sub", "leaf", None),
        P(None, "sub", "leaf", None),
        P("sub", "leaf", None, None),
        P(),
        P(),
    )
    out_specs = P(None, None, "sub", "leaf", None)
    return jax.shard_map(body, mesh=mesh, in_specs=in_specs, out_specs=out_specs, check_vma=False)
```

time: 163 us -> 143 us (0.88)
  the two profiles are of different devices: /device:TPU:18 before, /device:TPU:1 now
where the time goes in v1:
time: 143 us; the launch traced here: 142 us
  Pallas kernels  68 us (48%)
  waiting for transfers between devices  28.4 us (20%)
  starting transfers between devices  23.8 us (17%)
  matrix products  19.2 us (13%)
  local copies, waits for them, and re-layouts  1.75 us (1%)
    ppermute x7, waiting for transfers between devices, swapped(): return lax.ppermute(value, axis, pairs)  28.4 us
    pallas_call x1, Pallas kernels, own_near(): pl.pallas_call(own_kernel, grid=(points // (2 * SUB),), in_specs=[whole(a...  26.5 us
    pallas_call x1, Pallas kernels, prepare(): pl.pallas_call(prepare_kernel, grid=(rows // chunk,), in_specs=[pl.BlockS...  21.5 us
    pallas_call x1, Pallas kernels, finish(): pl.pallas_call(kernel, grid=(points // width,), in_specs=[whole(a) for a...  20 us
    ppermute x7, starting transfers between devices, swapped(): return lax.ppermute(value, axis, pairs)  15.5 us
    dot_general x13, matrix products, contract_last(): lax.dot_general(left_mat, right_mat, (((1,), (1,)), ((), ())), precision=...  10.6 us
    ppermute x1, starting transfers between devices, body(): left = lax.ppermute(tail, 'leaf', onward)  6.33 us
    dot_general x6, matrix products, lift_pair(): jnp.dot(right_part, transfer_pair[1], precision=PRECISE, preferred_elemen...  4.41 us
  transfers between devices with their start and end apart: 9, of which 5 were waited for; matrix products, arithmetic and copies ran while one was open for 12% of the time, Pallas kernels for 19%

profile of v1, /device:TPU:1, one launch (start us, length us, event | category | flops | bytes accessed | tf_op | source)
XLA Modules:
  0.0 142.3 jit_solution(1537510103094839006)
XLA Ops:
  0.0 21.5 %prepare.1 = (bf16[1024,2048]{1,0:T(8,128)(2,1)}, f8e4m3fn[1024,2048]{1,0:T(32,128)(4,1)}, f8e4m3fn[1024,2048]{1,0:T(32,128)(4,1)}, f32[1024,128]{1,0:T(8,128)},...) custom-call(f32[16384,128]{1,0:T(8,128)} %bitcast.93, ...), custom_call_target="tpu_custom_call" | custom-call | flops 14000000000 | bytes 28000000 | tf_op jit(solution)/shard_map/prepare/pallas_call | solution.py:171
  21.5 1.5 %collective-permute-start.2 = (f32[1024,64]{1,0:T(8,128)}, f32[1024,64]{1,0:T(8,128)S(1)}, u32[]{:S(2)}, u32[]{:S(2)}) collective-permute-start(f32[1024,64]{1,0:T(8,128)} %get-tuple-element.17), channel_id=1, source_target_pairs={{0,4},{4,0},{8,12},{12,8},{16,20},{20,16},{24,28},{28,24},{32,36},... | collective-permute-start | bytes 786440 | tf_op jit(solution)/shard_map/ppermute | solution.py:26
  23.0 1.7 %collective-permute-done.2 = f32[1024,64]{1,0:T(8,128)S(1)} collective-permute-done((f32[1024,64]{1,0:T(8,128)}, f32[1024,64]{1,0:T(8,128)S(1)}, u32[]{:S(2)}, u32[]{:S(2)}) %collective-permute-start.2) | collective-permute-done | bytes 262176 | tf_op jit(solution)/shard_map/ppermute | solution.py:26
  24.7 1.8 %fusion = f32[1024,64]{0,1:T(8,128)S(1)} fusion(f32[1024,64]{1,0:T(8,128)S(1)} %collective-permute-done.2, f32[1024,64]{1,0:T(8,128)} %get-tuple-element.17, pred[]{:T(512)S(6)} %eq.24, f32[7,2,64,64]{3,2,1,0:T(8,128)S(1)} %copy-done), kind=kOutput, calls=%fused_computation.13 | convolution fusion | flops 50397184 | bytes 1081345 | tf_op jit(solution)/shard_map/dot_general | solution.py:35
  26.5 0.7 convolution_add_fusion.11
  27.3 1.4 collective-permute-start.3
  28.6 6.2 %collective-permute-done.3 = f32[1024,64]{0,1:T(8,128)S(1)} collective-permute-done((f32[1024,64]{0,1:T(8,128)S(1)}, f32[1024,64]{0,1:T(8,128)S(1)}, u32[]{:S(2)}, u32[]{:S(2)}) %collective-permute-start.3) | collective-permute-done | bytes 262176 | tf_op jit(solution)/shard_map/ppermute | solution.py:26
  34.9 0.4 fusion.15
  35.3 0.4 convolution_add_fusion.10
  35.7 2.9 %collective-permute-start.4 = (f32[1024,64]{0,1:T(8,128)S(1)}, f32[1024,64]{0,1:T(8,128)S(1)}, u32[]{:S(2)}, u32[]{:S(2)}) collective-permute-start(f32[1024,64]{0,1:T(8,128)S(1)} %convolution_add_fusion.10), channel_id=1, source_target_pairs={{0,16},{4,20},{8,24},{12,28},{16,0},{20,4},{24,8},{28,12},{32,48},... | collective-permute-start | bytes 786440 | tf_op jit(solution)/shard_map/ppermute | solution.py:26
  38.6 5.3 %collective-permute-done.4 = f32[1024,64]{0,1:T(8,128)S(1)} collective-permute-done((f32[1024,64]{0,1:T(8,128)S(1)}, f32[1024,64]{0,1:T(8,128)S(1)}, u32[]{:S(2)}, u32[]{:S(2)}) %collective-permute-start.4) | collective-permute-done | bytes 262176 | tf_op jit(solution)/shard_map/ppermute | solution.py:26
  43.9 0.4 fusion.12
  44.3 0.4 convolution_add_fusion.9
  44.7 1.5 %collective-permute-start.5 = (f32[1024,64]{0,1:T(8,128)S(1)}, f32[1024,64]{0,1:T(8,128)S(1)}, u32[]{:S(2)}, u32[]{:S(2)}) collective-permute-start(f32[1024,64]{0,1:T(8,128)S(1)} %convolution_add_fusion.9), channel_id=1, source_target_pairs={{0,32},{4,36},{8,40},{12,44},{16,48},{20,52},{24,56},{28,60},{32,0... | collective-permute-start | bytes 786440 | tf_op jit(solution)/shard_map/ppermute | solution.py:26
  46.2 4.3 %collective-permute-done.5 = f32[1024,64]{0,1:T(8,128)S(1)} collective-permute-done((f32[1024,64]{0,1:T(8,128)S(1)}, f32[1024,64]{0,1:T(8,128)S(1)}, u32[]{:S(2)}, u32[]{:S(2)}) %collective-permute-start.5) | collective-permute-done | bytes 262176 | tf_op jit(solution)/shard_map/ppermute | solution.py:26
  50.5 0.4 fusion.9
  50.9 0.4 convolution_add_fusion.8
  51.3 3.1 %collective-permute-start.6 = (f32[1024,64]{0,1:T(8,128)S(1)}, f32[1024,64]{0,1:T(8,128)S(1)}, u32[]{:S(2)}, u32[]{:S(2)}) collective-permute-start(f32[1024,64]{0,1:T(8,128)S(1)} %convolution_add_fusion.8), channel_id=1, source_target_pairs={{0,64},{4,68},{8,72},{12,76},{16,80},{20,84},{24,88},{28,92},{32,9... | collective-permute-start | bytes 786440 | tf_op jit(solution)/shard_map/ppermute | solution.py:26
  54.4 6.3 %collective-permute-start = (f32[1032,512]{1,0:T(8,128)}, f32[1032,512]{1,0:T(8,128)}, u32[]{:S(2)}, u32[]{:S(2)}) collective-permute-start(f32[1032,512]{1,0:T(8,128)} %get-tuple-element.14), channel_id=1, source_target_pairs={{0,4},{4,8},{8,12},{12,16},{16,20},{20,24},{24,28},{28,32},{32,36}... | collective-permute-start | bytes 6340616 | tf_op jit(solution)/shard_map/ppermute | solution.py:398
  60.7 1.9 %collective-permute-start.1 = (f32[1032,512]{1,0:T(8,128)}, f32[1032,512]{1,0:T(8,128)}, u32[]{:S(2)}, u32[]{:S(2)}) collective-permute-start(f32[1032,512]{1,0:T(8,128)} %get-tuple-element.15), channel_id=1, source_target_pairs={{4,0},{8,4},{12,8},{16,12},{20,16},{24,20},{28,24},{32,28},{36,32}... | collective-permute-start | bytes 6340616 | tf_op jit(solution)/shard_map/ppermute | solution.py:399
  62.6 0.0 collective-permute-done.6
  62.7 0.4 fusion.6
  63.1 0.4 convolution_add_fusion.7
  63.5 1.9 %collective-permute-start.7 = (f32[1024,64]{0,1:T(8,128)S(1)}, f32[1024,64]{0,1:T(8,128)S(1)}, u32[]{:S(2)}, u32[]{:S(2)}) collective-permute-start(f32[1024,64]{0,1:T(8,128)S(1)} %convolution_add_fusion.7), channel_id=1, source_target_pairs={{0,1},{1,0},{2,3},{3,2},{4,5},{5,4},{6,7},{7,6},{8,9},{9,8},{10,11... | collective-permute-start | bytes 786440 | tf_op jit(solution)/shard_map/ppermute | solution.py:26
  65.4 26.5 %own_near.1.refs_5_ = f32[1024,2048]{1,0:T(8,128)} custom-call(bf16[1024,2048]{1,0:T(8,128)(2,1)} %get-tuple-element.18.qh_ref, f8e4m3fn[1024,2048]{1,0:T(32,128)(4,1)} %get-tuple-element.19.q8h_ref, f8e4m3fn[1024,2048]{1,0:T(32,128)(4,1)} %get-tuple-element.20.q8l_ref, f32[1024,128]{1,0:T(8,128)} %get-tuple-element.21.unit_ref, ...), custom_call_target="tpu_custom_call" | custom-call | flops 16999999488 | bytes 16000000 | tf_op jit(solution)/shard_map/own_near/pallas_call | solution.py:272
  91.9 1.0 fusion.3
  92.9 1.8 %convolution_add_fusion = f32[1024,64]{1,0:T(8,128)} fusion(f32[1024,64]{1,0:T(8,128)S(1)} %fusion.3, f32[1024,64]{0,1:T(8,128)S(1)} %convolution_add_fusion.7, f32[1024,64]{0,1:T(8,128)S(1)} %collective-permute-done.7, pred[]{:T(512)S(6)} %eq.29, f32[7,2,64,64]{3,2,1,0:T(8,128)S(1)} %copy-done), kind=kOutput, calls=%fused_computation | convolution fusion | flops 50462720 | bytes 1343489 | tf_op jit(solution)/shard_map/dot_general | solution.py:32
  94.7 3.3 %collective-permute-start.8 = (f32[1024,64]{1,0:T(8,128)}, f32[1024,64]{1,0:T(8,128)S(1)}, u32[]{:S(2)}, u32[]{:S(2)}) collective-permute-start(f32[1024,64]{1,0:T(8,128)} %convolution_add_fusion), channel_id=1, source_target_pairs={{0,2},{1,3},{2,0},{3,1},{4,6},{5,7},{6,4},{7,5},{8,10},{9,11},{10,... | collective-permute-start | bytes 786440 | tf_op jit(solution)/shard_map/ppermute | solution.py:26
  98.0 0.7 fusion.100
  98.7 0.9 multiply_reduce_fusion
  99.6 10.9 %collective-permute-done.8 = f32[1024,64]{1,0:T(8,128)S(1)} collective-permute-done((f32[1024,64]{1,0:T(8,128)}, f32[1024,64]{1,0:T(8,128)S(1)}, u32[]{:S(2)}, u32[]{:S(2)}) %collective-permute-start.8) | collective-permute-done | bytes 262176 | tf_op jit(solution)/shard_map/ppermute | solution.py:26
  110.5 0.6 convolution_add_fusion.6
  111.1 1.3 fusion.40
  112.4 1.0 convolution_add_fusion.1
  113.5 0.6 fusion.38
  114.0 1.0 convolution_add_fusion.2
  115.0 0.6 fusion.36
  115.6 1.0 convolution_add_fusion.3
  116.6 0.6 fusion.34
  117.2 1.0 convolution_add_fusion.4
  118.2 0.6 fusion.32
  118.8 1.0 convolution_add_fusion.5
  119.8 0.7 fusion.30
  120.5 0.7 convolution_add_fusion.12
  121.2 1.0 copy.10.refs_3_
  122.2 0.0 collective-permute-done.refs_0_
  122.3 0.0 collective-permute-done.1.refs_1_
  122.3 20.0 %finish.1 = f32[1024,2,8,128]{3,2,1,0:T(8,128)} custom-call(f32[1032,512]{1,0:T(8,128)} %collective-permute-done.refs_0_, f32[1032,512]{1,0:T(8,128)} %collective-permute-done.1.refs_1_, bf16[32,2048]{1,0:T(8,128)(2,1)} %get-tuple-element.16.target_ref.refs_2_, f32[1024,64]{1,0:T(8,128)} %copy.10.refs_3_, f32[64,2048]{1,0:T(8,128)} %bitcast.95, ...), custom_call_target="tpu_custom_call" | custom-call | flops 10000000000 | bytes 21000000 | tf_op jit(solution)/shard_map/finish/pallas_call | solution.py:357
  (8 shorter events, 0.0 us)
Async XLA Ops:
  0.0 24.7 %copy-start = (f32[7,2,64,64]{3,2,1,0:T(8,128)S(1)}, f32[7,2,64,64]{3,2,1,0:T(8,128)}, u32[]{:S(2)}) copy-start(f32[7,2,64,64]{3,2,1,0:T(8,128)} %param.10) | copy-start | bytes 688132
  21.5 3.2 %collective-permute-start.2 = (f32[1024,64]{1,0:T(8,128)}, f32[1024,64]{1,0:T(8,128)S(1)}, u32[]{:S(2)}, u32[]{:S(2)}) collective-permute-start(f32[1024,64]{1,0:T(8,128)} %get-tuple-element.17), channel_id=1, source_target_pairs={{0,4},{4,0},{8,12},{12,8},{16,20},{20,16},{24,28},{28,24},{32,36},... | collective-permute-start | bytes 786440 | tf_op jit(solution)/shard_map/ppermute | solution.py:26
  27.3 7.6 %collective-permute-start.3 = (f32[1024,64]{0,1:T(8,128)S(1)}, f32[1024,64]{0,1:T(8,128)S(1)}, u32[]{:S(2)}, u32[]{:S(2)}) collective-permute-start(f32[1024,64]{0,1:T(8,128)S(1)} %convolution_add_fusion.11), channel_id=1, source_target_pairs={{0,8},{4,12},{8,0},{12,4},{16,24},{20,28},{24,16},{28,20},{32,40},... | collective-permute-start | bytes 786440 | tf_op jit(solution)/shard_map/ppermute | solution.py:26
  35.7 8.2 %collective-permute-start.4 = (f32[1024,64]{0,1:T(8,128)S(1)}, f32[1024,64]{0,1:T(8,128)S(1)}, u32[]{:S(2)}, u32[]{:S(2)}) collective-permute-start(f32[1024,64]{0,1:T(8,128)S(1)} %convolution_add_fusion.10), channel_id=1, source_target_pairs={{0,16},{4,20},{8,24},{12,28},{16,0},{20,4},{24,8},{28,12},{32,48},... | collective-permute-start | bytes 786440 | tf_op jit(solution)/shard_map/ppermute | solution.py:26
  44.7 5.7 %collective-permute-start.5 = (f32[1024,64]{0,1:T(8,128)S(1)}, f32[1024,64]{0,1:T(8,128)S(1)}, u32[]{:S(2)}, u32[]{:S(2)}) collective-permute-start(f32[1024,64]{0,1:T(8,128)S(1)} %convolution_add_fusion.9), channel_id=1, source_target_pairs={{0,32},{4,36},{8,40},{12,44},{16,48},{20,52},{24,56},{28,60},{32,0... | collective-permute-start | bytes 786440 | tf_op jit(solution)/shard_map/ppermute | solution.py:26
  51.3 11.4 %collective-permute-start.6 = (f32[1024,64]{0,1:T(8,128)S(1)}, f32[1024,64]{0,1:T(8,128)S(1)}, u32[]{:S(2)}, u32[]{:S(2)}) collective-permute-start(f32[1024,64]{0,1:T(8,128)S(1)} %convolution_add_fusion.8), channel_id=1, source_target_pairs={{0,64},{4,68},{8,72},{12,76},{16,80},{20,84},{24,88},{28,92},{32,9... | collective-permute-start | bytes 786440 | tf_op jit(solution)/shard_map/ppermute | solution.py:26
  54.4 67.9 %collective-permute-start = (f32[1032,512]{1,0:T(8,128)}, f32[1032,512]{1,0:T(8,128)}, u32[]{:S(2)}, u32[]{:S(2)}) collective-permute-start(f32[1032,512]{1,0:T(8,128)} %get-tuple-element.14), channel_id=1, source_target_pairs={{0,4},{4,8},{8,12},{12,16},{16,20},{20,24},{24,28},{28,32},{32,36}... | collective-permute-start | bytes 6340616 | tf_op jit(solution)/shard_map/ppermute | solution.py:398
  60.7 61.5 %collective-permute-start.1 = (f32[1032,512]{1,0:T(8,128)}, f32[1032,512]{1,0:T(8,128)}, u32[]{:S(2)}, u32[]{:S(2)}) collective-permute-start(f32[1032,512]{1,0:T(8,128)} %get-tuple-element.15), channel_id=1, source_target_pairs={{4,0},{8,4},{12,8},{16,12},{20,16},{24,20},{28,24},{32,28},{36,32}... | collective-permute-start | bytes 6340616 | tf_op jit(solution)/shard_map/ppermute | solution.py:399
  63.5 28.4 %collective-permute-start.7 = (f32[1024,64]{0,1:T(8,128)S(1)}, f32[1024,64]{0,1:T(8,128)S(1)}, u32[]{:S(2)}, u32[]{:S(2)}) collective-permute-start(f32[1024,64]{0,1:T(8,128)S(1)} %convolution_add_fusion.7), channel_id=1, source_target_pairs={{0,1},{1,0},{2,3},{3,2},{4,5},{5,4},{6,7},{7,6},{8,9},{9,8},{10,11... | collective-permute-start | bytes 786440 | tf_op jit(solution)/shard_map/ppermute | solution.py:26
  91.9 7.7 %copy-start.1 = (f32[7,2,64,64]{3,2,1,0:T(8,128)S(1)}, f32[7,2,64,64]{3,2,1,0:T(8,128)}, u32[]{:S(2)}) copy-start(f32[7,2,64,64]{3,2,1,0:T(8,128)} %param.11) | copy-start | bytes 688132
  94.7 15.8 %collective-permute-start.8 = (f32[1024,64]{1,0:T(8,128)}, f32[1024,64]{1,0:T(8,128)S(1)}, u32[]{:S(2)}, u32[]{:S(2)}) collective-permute-start(f32[1024,64]{1,0:T(8,128)} %convolution_add_fusion), channel_id=1, source_target_pairs={{0,2},{1,3},{2,0},{3,1},{4,6},{5,7},{6,4},{7,5},{8,10},{9,11},{10,... | collective-permute-start | bytes 786440 | tf_op jit(solution)/shard_map/ppermute | solution.py:26
  99.6 13.9 %copy-start.2 = (f32[1,2,64,64]{3,2,1,0:T(8,128)S(1)}, f32[1,2,64,64]{3,2,1,0:T(8,128)}, u32[]{:S(2)}) copy-start(f32[1,2,64,64]{3,2,1,0:T(8,128)} %get-tuple-element.33) | copy-start | bytes 98308

commit v2 on v1

--- a/solution.py
+++ b/solution.py
@@ -6,7 +6,6 @@
 from jax.sharding import PartitionSpec as P
 
 DELTA_SQ = 0.0025
-PRECISE = lax.Precision.HIGHEST
 F8 = jnp.float8_e4m3fn
 BF = jnp.bfloat16
 F32 = jnp.float32
@@ -18,33 +17,6 @@
 LANES = 128
 PAD = 8
 LIMIT = 60 * 1024 * 1024
-
-
-def swapped(value, axis, stride):
-    mask = 2**stride
-    pairs = [(source, source ^ mask) for source in range(lax.axis_size(axis))]
-    return lax.ppermute(value, axis, pairs)
-
-
-def lift_pair(current, sibling, branch_bit, transfer_pair):
-    left_part = jnp.where(branch_bit == 0, current, sibling)
-    right_part = jnp.where(branch_bit == 0, sibling, current)
-    parent = jnp.dot(
-        left_part, transfer_pair[0], precision=PRECISE, preferred_element_type=jnp.float32
-    )
-    return parent + jnp.dot(
-        right_part, transfer_pair[1], precision=PRECISE, preferred_element_type=jnp.float32
-    )
-
-
-def contract_last(left_mat, right_mat):
-    return lax.dot_general(
-        left_mat,
-        right_mat,
-        (((1,), (1,)), ((), ())),
-        precision=PRECISE,
-        preferred_element_type=jnp.float32,
-    )
 
 
 def mm(left, right):
@@ -217,7 +189,7 @@
         w8l[slot, rows, :] = (weight - high.astype(F32)).astype(F8)
 
 
-def sweep(source_ref, target_ref, row_count, w, w8h, w8l, emit, count):
+def sweep(source_ref, target_ref, row_count, w, w8h, w8l, emit, count, between=None):
     points = source_ref.shape[0]
     blocks = target_ref.shape[1] // SUB
     step = pl.program_id(0)
@@ -246,16 +218,254 @@
                 w8l,
             )
             emit(slice(part * height, (part + 1) * height), block, slot)
-
-
-def own_kernel(qh_ref, q8h_ref, q8l_ref, unit_ref, source_ref, target_ref, out_ref, w, w8h, w8l):
+        if between is not None:
+            between(step, block)
+
+
+def fine(left, right, product):
+    left_high, left_low = split(left)
+    right_high, right_low = split(right)
+    low = product(left_low.astype(BF), right_high) + product(left_high, right_low.astype(BF))
+    return product(left_high, right_high) + low
+
+
+class Stage:
+    def __init__(self, axis, shift, bits, level, rows):
+        self.axis = axis
+        self.shift = shift
+        self.bits = bits
+        self.level = level
+        self.size = 1 << bits
+        self.rows = rows
+        self.share = rows // self.size
+
+    def scratch(self, rank):
+        return [
+            pltpu.VMEM((self.size, self.share, rank), F32),
+            pltpu.VMEM((self.size, self.share, rank), F32),
+            pltpu.VMEM((self.size, self.share, rank), F32),
+            pltpu.VMEM((self.size, self.share, rank), F32),
+            pltpu.VMEM((self.share, rank), F32),
+        ] + [pltpu.SemaphoreType.DMA((self.size - 1,))] * 4
+
+    def place(self):
+        position = lax.axis_index(self.axis)
+        member = lax.rem(position // (1 << self.shift), self.size)
+        return position, member
+
+    def partner(self, offset):
+        position, member = self.place()
+        peer = lax.rem(member + offset, self.size)
+        return peer, {self.axis: position + (peer - member) * (1 << self.shift)}
+
+    def bind(self, refs):
+        self.gathered, self.middle, self.outgoing, self.returned, self.top = refs[:5]
+        self.semaphores = refs[5:]
+
+    def upward(self, source):
+        _, member = self.place()
+        out = []
+        for offset in range(1, self.size):
+            peer, device = self.partner(offset)
+            rows = pl.ds(pl.multiple_of(peer * self.share, self.share), self.share)
+            out.append(
+                pltpu.make_async_remote_copy(
+                    src_ref=source.at[rows, :],
+                    dst_ref=self.gathered.at[member],
+                    send_sem=self.semaphores[0].at[offset - 1],
+                    recv_sem=self.semaphores[1].at[offset - 1],
+                    device_id=device,
+                    device_id_type=pl.DeviceIdType.MESH,
+                )
+            )
+        return out
+
+    def downward(self):
+        _, member = self.place()
+        out = []
+        for offset in range(1, self.size):
+            peer, device = self.partner(offset)
+            out.append(
+                pltpu.make_async_remote_copy(
+                    src_ref=self.outgoing.at[peer],
+                    dst_ref=self.returned.at[member],
+                    send_sem=self.semaphores[2].at[offset - 1],
+                    recv_sem=self.semaphores[3].at[offset - 1],
+                    device_id=device,
+                    device_id_type=pl.DeviceIdType.MESH,
+                )
+            )
+        return out
+
+    def send_up(self, source):
+        for copy in self.upward(source):
+            copy.start()
+        _, member = self.place()
+        rows = pl.ds(pl.multiple_of(member * self.share, self.share), self.share)
+        self.gathered[member] = source[rows, :]
+
+    def send_down(self):
+        for copy in self.downward():
+            copy.start()
+        _, member = self.place()
+        self.returned[member] = self.outgoing[member]
+
+    def levels(self, source, transfer_ref, last):
+        for copy in self.upward(source):
+            copy.wait_recv()
+        nodes = [self.gathered[index] for index in range(self.size)]
+        first = 0
+        for step in range(self.bits):
+            if last and step == self.bits - 1:
+                break
+            level = self.level + step
+            even = jnp.concatenate(nodes[0::2], axis=0)
+            odd = jnp.concatenate(nodes[1::2], axis=0)
+            parents = fine(even, transfer_ref[level, 0], mm) + fine(odd, transfer_ref[level, 1], mm)
+            nodes = [
+                parents[index * self.share : (index + 1) * self.share]
+                for index in range(len(nodes) // 2)
+            ]
+            if step < self.bits - 1:
+                for index, value in enumerate(nodes):
+                    self.middle[first + index] = value
+                first += len(nodes)
+            else:
+                self.top[...] = nodes[0]
+
+    def expand(self, parent, transfer_ref, coupling_ref):
+        expansions = [parent]
+        starts = []
+        first = 0
+        for step in range(1, self.bits):
+            starts.append(first)
+            first += self.size >> step
+        for step in reversed(range(self.bits)):
+            level = self.level + step
+            held = self.gathered if step == 0 else self.middle
+            base = 0 if step == 0 else starts[step - 1]
+            count = self.size >> step
+            results = [None] * count
+            for side in range(2):
+                sibling = jnp.concatenate(
+                    [held[base + index] for index in range(1 - side, count, 2)], axis=0
+                )
+                value = fine(sibling, coupling_ref[level, side], mm_nt)
+                if expansions[0] is not None:
+                    above = jnp.concatenate(expansions, axis=0)
+                    value = value + fine(above, transfer_ref[level, side], mm_nt)
+                for index in range(count // 2):
+                    results[2 * index + side] = value[
+                        index * self.share : (index + 1) * self.share
+                    ]
+            expansions = results
+        for index, value in enumerate(expansions):
+            self.outgoing[index] = value
+
+    def arrived(self):
+        for copy in self.downward():
+            copy.wait_recv()
+        return jnp.concatenate([self.returned[index] for index in range(self.size)], axis=0)
+
+    def sent(self, source):
+        for copy in self.upward(source) + self.downward():
+            copy.wait_send()
+
+
+def own_kernel(
+    stages, qh_ref, q8h_ref, q8l_ref, unit_ref, source_ref, target_ref, moment_ref, transfer_ref,
+    coupling_ref, tail_ref, head_ref, out_ref, expansion_ref, left_ref, right_ref,
+    w, w8h, w8l, edge_sems, *stage_refs,
+):
+    per_stage = len(stage_refs) // len(stages)
+    for index, stage in enumerate(stages):
+        stage.bind(stage_refs[index * per_stage : (index + 1) * per_stage])
+    low, middle, high = stages
+    position = lax.axis_index("leaf")
+    count = lax.axis_size("leaf")
+    after = {"leaf": lax.rem(position + 1, count)}
+    before = {"leaf": lax.rem(position + count - 1, count)}
+
+    def edges():
+        return [
+            pltpu.make_async_remote_copy(
+                src_ref=source,
+                dst_ref=target,
+                send_sem=edge_sems.at[index],
+                recv_sem=edge_sems.at[2 + index],
+                device_id=device,
+                device_id_type=pl.DeviceIdType.MESH,
+            )
+            for index, (source, target, device) in enumerate(
+                ((tail_ref, left_ref, after), (head_ref, right_ref, before))
+            )
+        ]
+
+    @pl.when(pl.program_id(0) == 0)
+    def _():
+        barrier = pltpu.get_barrier_semaphore()
+        devices = [before, after]
+        for stage in stages:
+            devices += [stage.partner(offset)[1] for offset in range(1, stage.size)]
+        for device in devices:
+            pl.semaphore_signal(
+                barrier, inc=1, device_id=device, device_id_type=pl.DeviceIdType.MESH
+            )
+        pl.semaphore_wait(barrier, len(devices))
+        low.send_up(moment_ref)
+        for copy in edges():
+            copy.start()
+
     def emit(rows, block, slot):
         total = mm(qh_ref[rows, :], w[slot])
         total = total + mm(q8h_ref[rows, :], w8l[slot])
         total = total + mm(q8l_ref[rows, :], w8h[slot])
         out_ref[rows, block * SUB : (block + 1) * SUB] = total * unit_ref[rows, 0:1]
 
-    sweep(source_ref, target_ref, out_ref.shape[0], w, w8h, w8l, emit, 2)
+    def between(step, block):
+        def at(number):
+            return pl.when(step == number)
+
+        if block == 1:
+
+            @at(0)
+            def _():
+                low.levels(moment_ref, transfer_ref, False)
+                middle.send_up(low.top)
+
+            @at(1)
+            def _():
+                high.levels(middle.top, transfer_ref, True)
+                high.expand(None, transfer_ref, coupling_ref)
+                high.send_down()
+
+            @at(2)
+            def _():
+                low.expand(middle.arrived(), transfer_ref, coupling_ref)
+                low.send_down()
+
+            @at(3)
+            def _():
+                expansion_ref[...] = low.arrived()
+                low.sent(moment_ref)
+                middle.sent(low.top)
+                high.sent(middle.top)
+                for copy in edges():
+                    copy.wait()
+
+        else:
+
+            @at(1)
+            def _():
+                middle.levels(low.top, transfer_ref, False)
+                high.send_up(middle.top)
+
+            @at(2)
+            def _():
+                middle.expand(high.arrived(), transfer_ref, coupling_ref)
+                middle.send_down()
+
+    sweep(source_ref, target_ref, out_ref.shape[0], w, w8h, w8l, emit, 2, between)
 
 
 def weight_scratch(count):
@@ -266,26 +476,60 @@
     ]
 
 
-def own_near(high, high8, low8, unit, source, target):
+def own_near(high, high8, low8, unit, source, target, moment, transfer, coupling, tail, head):
     rows, points = high.shape
-    whole = lambda a: pl.BlockSpec(a.shape, lambda step: (0, 0), pipeline_mode=pl.Buffered(1))
+    rank = moment.shape[1]
+    leaf_bits = lax.axis_size("leaf").bit_length() - 1
+    sub_bits = lax.axis_size("sub").bit_length() - 1
+    near_bits = leaf_bits - leaf_bits // 2
+    stages = []
+    height = rows
+    level = 0
+    for axis, shift, bits in (
+        ("leaf", 0, near_bits),
+        ("leaf", near_bits, leaf_bits - near_bits),
+        ("sub", 0, sub_bits),
+    ):
+        stages.append(Stage(axis, shift, bits, level, height))
+        level += bits
+        height = stages[-1].share
+    whole = lambda a: pl.BlockSpec(
+        a.shape, lambda step: (0,) * len(a.shape), pipeline_mode=pl.Buffered(1)
+    )
+    far = pl.BlockSpec(memory_space=pl.ANY)
+    near = (high, high8, low8, unit, source, target, moment, transfer, coupling)
+    scratch = []
+    for stage in stages:
+        scratch += stage.scratch(rank)
     return pl.pallas_call(
-        own_kernel,
+        lambda *refs: own_kernel(stages, *refs),
         grid=(points // (2 * SUB),),
-        in_specs=[whole(a) for a in (high, high8, low8, unit, source, target)],
-        out_specs=pl.BlockSpec((rows, 2 * SUB), lambda step: (0, step)),
-        out_shape=jax.ShapeDtypeStruct((rows, points), F32),
-        scratch_shapes=weight_scratch(points),
-        compiler_params=pltpu.CompilerParams(vmem_limit_bytes=LIMIT),
+        in_specs=[whole(a) for a in near] + [far, far],
+        out_specs=[
+            pl.BlockSpec((rows, 2 * SUB), lambda step: (0, step)),
+            pl.BlockSpec((rows, rank), lambda step: (0, 0)),
+            far,
+            far,
+        ],
+        out_shape=[
+            jax.ShapeDtypeStruct((rows, points), F32),
+            jax.ShapeDtypeStruct((rows, rank), F32),
+            jax.ShapeDtypeStruct(tail.shape, F32),
+            jax.ShapeDtypeStruct(head.shape, F32),
+        ],
+        scratch_shapes=weight_scratch(points) + [pltpu.SemaphoreType.DMA((4,))] + scratch,
+        compiler_params=pltpu.CompilerParams(
+            vmem_limit_bytes=LIMIT, collective_id=0, has_side_effects=True
+        ),
         cost_estimate=pl.CostEstimate(
-            flops=17_000_000_000, bytes_accessed=16_000_000, transcendentals=4_000_000
+            flops=17_000_000_000, bytes_accessed=24_000_000, transcendentals=4_000_000
         ),
         name="own_near",
-    )(high, high8, low8, unit, source, target)
+    )(*near, tail, head)
 
 
 def rest_kernel(
-    factor, left_ref, right_ref, target_ref, expansion_ref, bases_ref, near_ref,
+    factor, left_ref, right_ref, edge_ref, target_ref, expansion_ref, bases_ref, near_ref,
     out_ref, qh, q8h, q8l, units, far, basis, source_rows, source, w, w8h, w8l,
 ):
     strip = left_ref.shape[1]
@@ -306,7 +550,10 @@
         @pl.loop(0, row_count // SUB)
         def _(step):
             rows = pl.ds(pl.multiple_of(step * SUB, SUB), SUB)
-            joined = jnp.concatenate([left_ref[rows, :], right_ref[rows, :]], axis=1)
+            joined = jnp.concatenate(
+                [left_ref[rows, :] * edge_ref[0:1, 0:1], right_ref[rows, :] * edge_ref[1:2, 0:1]],
+                axis=1,
+            )
             full, high, rest, unit = scaled(joined)
             qh[rows, :] = high
             q8h[rows, :] = full.astype(F8)
@@ -342,7 +589,7 @@
     sweep(source, target_ref, row_count, w, w8h, w8l, emit, OUT_BLOCKS)
 
 
-def finish(left, right, target, expansion, bases, near, factor):
+def finish(left, right, edge, target, expansion, bases, near, factor):
     rows, points = near.shape
     strip = left.shape[1]
     rank = bases.shape[0]
@@ -350,14 +597,14 @@
     whole = lambda a: pl.BlockSpec(a.shape, lambda step: (0, 0), pipeline_mode=pl.Buffered(1))
 
     def kernel(*refs):
-        out = refs[6]
+        out = refs[7]
         flat = out.reshape(rows * PAD, LANES)
-        rest_kernel(factor, *refs[:6], flat, *refs[7:])
+        rest_kernel(factor, *refs[:7], flat, *refs[8:])
 
     return pl.pallas_call(
         kernel,
         grid=(points // width,),
-        in_specs=[whole(a) for a in (left, right, target, expansion, bases)]
+        in_specs=[whole(a) for a in (left, right, edge, target, expansion, bases)]
         + [pl.BlockSpec((rows, width), lambda step: (0, step))],
         out_specs=pl.BlockSpec((rows, 1, PAD, LANES), lambda step: (0, step, 0, 0)),
         out_shape=jax.ShapeDtypeStruct((rows, points // width, PAD, LANES), F32),
@@ -377,7 +624,7 @@
             flops=10_000_000_000, bytes_accessed=21_000_000, transcendentals=2_000_000
         ),
         name="finish",
-    )(left, right, target, expansion, bases, near)
+    )(left, right, edge, target, expansion, bases, near)
 
 
 def body(charges, ordering, jitter, leaf_bases, transfer, coupling):
@@ -392,45 +639,14 @@
         jitter.reshape(3, 1, points),
         leaf_basis,
     )
-    count = lax.axis_size("leaf")
-    onward = [(i, i + 1) for i in range(count - 1)]
-    back = [(i + 1, i) for i in range(count - 1)]
-    left = lax.ppermute(tail, "leaf", onward)
-    right = lax.ppermute(head, "leaf", back)
-    near_part = own_near(high, high8, low8, unit, own_source, target_rows)
-    leaf_levels = lax.axis_size("leaf").bit_length() - 1
-    sub_levels = lax.axis_size("sub").bit_length() - 1
+    near_part, expansion, left, right = own_near(
+        high, high8, low8, unit, own_source, target_rows, moment, transfer, coupling, tail, head
+    )
     position = lax.axis_index("leaf")
-    siblings = []
-    branch_bits = []
-    current = moment
-    for bit_index in range(leaf_levels):
-        sibling = swapped(current, "leaf", bit_index)
-        branch_bit = position >> bit_index & 1
-        current = lift_pair(current, sibling, branch_bit, transfer[bit_index])
-        siblings.append(sibling)
-        branch_bits.append(branch_bit)
-    sub_position = lax.axis_index("sub")
-    for bit_index in range(sub_levels):
-        level_index = leaf_levels + bit_index
-        sibling = swapped(current, "sub", bit_index)
-        branch_bit = sub_position >> bit_index & 1
-        current = lift_pair(current, sibling, branch_bit, transfer[level_index])
-        siblings.append(sibling)
-        branch_bits.append(branch_bit)
-    expansion = jnp.zeros((row_count, moment.shape[1]), jnp.float32)
-    for level_index in reversed(range(leaf_levels + sub_levels)):
-        couple_mat = lax.dynamic_index_in_dim(
-            coupling[level_index], branch_bits[level_index], 0, keepdims=False
-        )
-        transfer_mat = lax.dynamic_index_in_dim(
-            transfer[level_index], branch_bits[level_index], 0, keepdims=False
-        )
-        expansion = contract_last(siblings[level_index], couple_mat) + contract_last(
-            expansion, transfer_mat
-        )
+    inner = jnp.stack([position > 0, position < lax.axis_size("leaf") - 1])
+    edge = jnp.broadcast_to(inner[:, None].astype(F32), (2, LANES))
     potential = finish(
-        left, right, target_rows, expansion, leaf_basis, near_part, near_scale / GAIN
+        left, right, edge, target_rows, expansion, leaf_basis, near_part, near_scale / GAIN
     )
     return potential.reshape(set_count, vector_count, 1, 1, points)
 

time: 143 us -> 105 us (0.73)
  Pallas kernels: 68 us -> 103 us
  waiting for transfers between devices: 28.4 us -> 0 us
  starting transfers between devices: 23.8 us -> 0 us
  matrix products: 19.2 us -> 0 us
    pallas_call x1, Pallas kernels: 26.5 us -> 62.1 us  [own_near(): pl.pallas_call(lambda *refs: own_kernel(stages, *refs), grid=(points // (...]
    ppermute x9 -> x0, waiting for transfers between devices: 28.4 us -> none  [the longest x7 28.4 us: swapped(): return lax.ppermute(value, axis, pairs)]
    ppermute x9 -> x0, starting transfers between devices: 23.8 us -> none  [the longest x7 15.5 us: swapped(): return lax.ppermute(value, axis, pairs)]
    dot_general x25 -> x0, matrix products: 19.2 us -> none  [the longest x13 10.6 us: contract_last(): lax.dot_general(left_mat, right_mat, (((1,), (1,)), ((), ())), precision=...]
  transfers between devices with their start and end apart: 9 -> 0, of which waited for: 5 -> 0; matrix products, arithmetic and copies ran while one was open for 12% -> 0% of each run, Pallas kernels for 19% -> 0%
where the time goes in v2:
time: 105 us; the launch traced here: 104 us
  Pallas kernels  103 us (98%)
    pallas_call x1, Pallas kernels, own_near(): pl.pallas_call(lambda *refs: own_kernel(stages, *refs), grid=(points // (...  62.1 us
    pallas_call x1, Pallas kernels, prepare(): pl.pallas_call(prepare_kernel, grid=(rows // chunk,), in_specs=[pl.BlockS...  21.4 us
    pallas_call x1, Pallas kernels, finish(): pl.pallas_call(kernel, grid=(points // width,), in_specs=[whole(a) for a...  20 us

profile of v2, /device:TPU:1, one launch (start us, length us, event | category | flops | bytes accessed | tf_op | source)
XLA Modules:
  0.0 104.2 jit_solution(14590712952616135770)
XLA Ops:
  0.0 21.4 %prepare.1 = (bf16[1024,2048]{1,0:T(8,128)(2,1)}, f8e4m3fn[1024,2048]{1,0:T(32,128)(4,1)}, f8e4m3fn[1024,2048]{1,0:T(32,128)(4,1)}, f32[1024,128]{1,0:T(8,128)},...) custom-call(f32[16384,128]{1,0:T(8,128)} %bitcast.7, ...), custom_call_target="tpu_custom_call" | custom-call | flops 14000000000 | bytes 28000000 | tf_op jit(solution)/shard_map/prepare/pallas_call | solution.py:143
  21.4 62.1 %own_near.1 = (f32[1024,2048]{1,0:T(8,128)}, f32[1024,64]{1,0:T(8,128)}, f32[1032,512]{1,0:T(8,128)}, f32[1032,512]{1,0:T(8,128)}) custom-call(bf16[1024,2048]{1,0:T(8,128)(2,1)} %get-tuple-element.18.refs_0_, f8e4m3fn[1024,2048]{1,0:T(32,128)(4,1)} %get-tuple-element.19.refs_1_, f8e4m3fn[1024,2048]{1,0:T(32,128)(4,1)} %get-tuple-element.20.refs_2_, ...), custom_call_target="tpu_custom_call" | custom-call | flops 16999999488 | bytes 24000000 | tf_op jit(solution)/shard_map/own_near/pallas_call | solution.py:504
  83.5 0.1 add_convert_fusion
  83.6 0.6 broadcast_in_dim.2.refs_2_
  84.2 20.0 %finish.1 = f32[1024,2,8,128]{3,2,1,0:T(8,128)} custom-call(f32[1032,512]{1,0:T(8,128)} %get-tuple-element.27.refs_0_, f32[1032,512]{1,0:T(8,128)} %get-tuple-element.28.refs_1_, f32[2,128]{1,0:T(2,128)} %broadcast_in_dim.2.refs_2_, bf16[32,2048]{1,0:T(8,128)(2,1)} %get-tuple-element.23.refs_5_.refs_3_, f32[1024,64]{1,0:T(8,128)} %get-tuple-element.29.refs_4_, ...), custom_call_target="tpu_custom_call" | custom-call | flops 10000000000 | bytes 21000000 | tf_op jit(solution)/shard_map/finish/pallas_call | solution.py:604

commit v3 on v2

v3 whole, which is shorter than its diff:
```python
import jax
import jax.numpy as jnp
from jax import lax
from jax.experimental import pallas as pl
from jax.experimental.pallas import tpu as pltpu
from jax.sharding import PartitionSpec as P

DELTA_SQ = 0.0025
F8 = jnp.float8_e4m3fn
BF = jnp.bfloat16
F32 = jnp.float32
GAIN = 16.0
TOP = 384.0
FEATS = 32
SUB = 256
OUT_BLOCKS = 4
LANES = 128
PAD = 8
LIMIT = 60 * 1024 * 1024


def mm(left, right):
    return jnp.dot(left, right, preferred_element_type=F32)


def mm_nt(left, right):
    return lax.dot_general(left, right, (((1,), (1,)), ((), ())), preferred_element_type=F32)


def split(value):
    high = value.astype(BF)
    return high, value - high.astype(F32)


def features(coords, source_ref, target_ref, columns):
    ones = jnp.ones_like(coords[0])
    norm = sum(coord * coord for coord in coords)

    def pieces(value):
        out = []
        for _ in range(3):
            high, value = split(value)
            out.append(high.astype(F32))
        return out

    source = []
    target = []
    for coord in coords:
        part = pieces(coord)
        for left, right in ((0, 0), (0, 1), (1, 0), (1, 1), (0, 2), (2, 0)):
            source.append(part[left])
            target.append(-2.0 * part[right])
    source += pieces(norm + DELTA_SQ / (GAIN * GAIN)) + [ones] * 3
    target += [ones] * 3 + pieces(norm)
    blank = [jnp.zeros_like(norm)] * (FEATS - len(source))
    for ref, rows in ((source_ref, source + blank), (target_ref, target + blank)):
        if ref is not None:
            for index, row in enumerate(rows):
                ref[index : index + 1, columns] = row


def scaled(rows):
    top = jnp.maximum(jnp.max(jnp.abs(rows), axis=1, keepdims=True), 1e-30)
    full = rows * (TOP / top)
    high = full.astype(BF)
    return full, high, full - high.astype(F32), top * (1.0 / TOP)


def weigh(source_ref, target, first, last, slot, w, w8h, w8l):
    for row in range(first, last, 128):
        rows = slice(row, row + 128)
        weight = lax.rsqrt(mm(source_ref[rows, :], target))
        high = weight.astype(BF)
        w[slot, rows, :] = high
        w8h[slot, rows, :] = weight.astype(F8)
        w8l[slot, rows, :] = (weight - high.astype(F32)).astype(F8)


def sweep(source_ref, target_ref, row_count, w, w8h, w8l, emit, count, step):
    points = source_ref.shape[0]
    blocks = target_ref.shape[1] // SUB
    parts = 4

    def target(block):
        return target_ref[:, pl.ds(pl.multiple_of(block * SUB, SUB), SUB)]

    @pl.when(step == 0)
    def _():
        weigh(source_ref, target(0), 0, points, 0, w, w8h, w8l)

    height = row_count // parts
    for block in range(count):
        slot = block % 2
        coming = target(jnp.minimum(count * step + block + 1, blocks - 1))
        for part in range(parts):
            weigh(
                source_ref,
                coming,
                part * points // parts,
                (part + 1) * points // parts,
                1 - slot,
                w,
                w8h,
                w8l,
            )
            emit(slice(part * height, (part + 1) * height), block, slot)


def fine(left, right, product):
    left_high, left_low = split(left)
    right_high, right_low = split(right)
    low = product(left_low.astype(BF), right_high) + product(left_high, right_low.astype(BF))
    return product(left_high, right_high) + low


def pack(value):
    half = value.shape[0] // 2
    return jnp.concatenate([value[:half], value[half:]], axis=1)


def unpack(value):
    half = value.shape[1] // 2
    return jnp.concatenate([value[:, :half], value[:, half:]], axis=0)


class Stage:
    def __init__(self, axis, shift, bits, level):
        self.axis = axis
        self.shift = shift
        self.bits = bits
        self.level = level
        self.size = 1 << bits

    def scratch(self, share, rank):
        width = (share // 2, 2 * rank)
        count = self.size - 1
        return [
            pltpu.VMEM((self.size,) + width, F32),
            pltpu.VMEM((max(self.size - 2, 1), share, rank), F32),
            pltpu.VMEM((self.size,) + width, F32),
            pltpu.VMEM((self.size,) + width, F32),
            pltpu.VMEM(width, F32),
        ] + [pltpu.SemaphoreType.DMA((count,))] * 4

    def bind(self, refs):
        self.gathered, self.middle, self.outgoing, self.returned, self.top = refs[:5]
        self.semaphores = refs[5:]

    def member(self):
        return lax.rem(lax.axis_index(self.axis) // (1 << self.shift), self.size)

    def partner(self, offset):
        position = lax.axis_index(self.axis)
        peer = lax.rem(self.member() + offset, self.size)
        return peer, {self.axis: position + (peer - self.member()) * (1 << self.shift)}

    def copies(self, source, target, sems):
        out = []
        for offset in range(1, self.size):
            peer, device = self.partner(offset)
            out.append(
                pltpu.make_async_remote_copy(
                    src_ref=source.at[peer] if len(source.shape) == 3 else source,
                    dst_ref=target.at[self.member()],
                    send_sem=self.semaphores[sems].at[offset - 1],
                    recv_sem=self.semaphores[sems + 1].at[offset - 1],
                    device_id=device,
                    device_id_type=pl.DeviceIdType.MESH,
                )
            )
        return out

    def upward(self, source):
        return self.copies(source, self.gathered, 0)

    def downward(self):
        return self.copies(self.outgoing, self.returned, 2)

    def send_up(self, source):
        for copy in self.upward(source):
            copy.start()
        member = self.member()
        self.gathered[member] = source[member] if len(source.shape) == 3 else source[...]

    def send_down(self):
        for copy in self.downward():
            copy.start()
        member = self.member()
        self.returned[member] = self.outgoing[member]

    def levels(self, source, transfer_ref, last):
        for copy in self.upward(source):
            copy.wait_recv()
        share = self.middle.shape[1]
        nodes = [unpack(self.gathered[index]) for index in range(self.size)]
        first = 0
        for step in range(self.bits - 1 if last else self.bits):
            level = self.level + step
            even = jnp.concatenate(nodes[0::2], axis=0)
            odd = jnp.concatenate(nodes[1::2], axis=0)
            parents = fine(even, transfer_ref[level, 0], mm) + fine(odd, transfer_ref[level, 1], mm)
            nodes = [
                parents[index * share : (index + 1) * share] for index in range(len(nodes) // 2)
            ]
            if step < self.bits - 1:
                for index, value in enumerate(nodes):
                    self.middle[first + index] = value
                first += len(nodes)
            else:
                self.top[...] = pack(nodes[0])

    def expand(self, parent, transfer_ref, coupling_ref):
        share = self.middle.shape[1]
        expansions = [parent]
        starts = [0]
        for step in range(1, self.bits):
            starts.append(starts[-1] + (self.size >> step))
        for step in reversed(range(self.bits)):
            level = self.level + step
            count = self.size >> step
            if step == 0:
                held = [unpack(self.gathered[index]) for index in range(count)]
            else:
                held = [self.middle[starts[step - 1] + index] for index in range(count)]
            results = [None] * count
            for side in range(2):
                sibling = jnp.concatenate(held[1 - side :: 2], axis=0)
                value = fine(sibling, coupling_ref[level, side], mm_nt)
                if expansions[0] is not None:
                    above = jnp.concatenate(expansions, axis=0)
                    value = value + fine(above, transfer_ref[level, side], mm_nt)
                for index in range(count // 2):
                    results[2 * index + side] = value[index * share : (index + 1) * share]
            expansions = results
        for index, value in enumerate(expansions):
            self.outgoing[index] = pack(value)

    def chosen(self):
        return unpack(self.outgoing[self.member()])

    def arrived(self):
        for copy in self.downward():
            copy.wait_recv()
        return jnp.concatenate([unpack(self.returned[i]) for i in range(self.size)], axis=0)


def own_kernel(
    stages, q_ref, order_ref, jitter_ref, bases_ref, transfer_ref, coupling_ref,
    out_ref, target_out, expansion_ref, left_ref, right_ref,
    pick, pick8, basis, moved, source_rows, target_rows, feat, target, qh, q8h, q8l, unit_ref,
    tail, head, packed, edge_sems, w, w8h, w8l, *stage_refs,
):
    per_stage = len(stage_refs) // len(stages)
    for index, stage in enumerate(stages):
        stage.bind(stage_refs[index * per_stage : (index + 1) * per_stage])
    low, middle, high = stages
    points = order_ref.shape[1]
    strip = tail.shape[1]
    rank = bases_ref.shape[0]
    row_count = qh.shape[0]
    tiles = points // LANES
    chunk = q_ref.shape[0] // tiles
    chunks = row_count // chunk
    last = points - strip
    now = pl.program_id(0)
    position = lax.axis_index("leaf")
    count = lax.axis_size("leaf")
    after = {"leaf": lax.rem(position + 1, count)}
    before = {"leaf": lax.rem(position + count - 1, count)}

    def edges(first, height, slot):
        rows = pl.ds(first, height)
        return [
            pltpu.make_async_remote_copy(
                src_ref=source.at[rows, :],
                dst_ref=target.at[rows, :],
                send_sem=edge_sems.at[2 * index, slot],
                recv_sem=edge_sems.at[2 * index + 1, slot],
                device_id=device,
                device_id_type=pl.DeviceIdType.MESH,
            )
            for index, (source, target, device) in enumerate(
                ((tail, left_ref, after), (head, right_ref, before))
            )
        ]

    @pl.when(now == 0)
    def _():
        barrier = pltpu.get_barrier_semaphore()
        devices = [before, after]
        for stage in stages:
            devices += [stage.partner(offset)[1] for offset in range(1, stage.size)]
        for device in devices:
            pl.semaphore_signal(
                barrier, inc=1, device_id=device, device_id_type=pl.DeviceIdType.MESH
            )

        index = lax.broadcasted_iota(jnp.int32, (1, points), 1).astype(F32)
        coords = [(index + jitter_ref[0]) * (1.0 / points), jitter_ref[1], jitter_ref[2]]
        coords = [(coord - 0.5) * (1.0 / GAIN) for coord in coords]
        features(coords, source_rows, target_rows, slice(0, points))
        target[...] = target_rows[...].astype(BF)
        target_out[...] = target_rows[...].astype(BF)
        for axis in range(3):
            tail[row_count + axis : row_count + axis + 1, :] = coords[axis][:, last:]
            head[row_count + axis : row_count + axis + 1, :] = coords[axis][:, :strip]
        blank = jnp.zeros((PAD - 3, strip), F32)
        tail[row_count + 3 :, :] = blank
        head[row_count + 3 :, :] = blank
        top, rest = split(bases_ref[...])
        moved[:rank, :] = top
        moved[rank : 2 * rank, :] = rest.astype(BF)
        moved[2 * rank :, :] = source_rows[...].astype(BF)

        @pl.loop(0, points // SUB)
        def _(step):
            rows = pl.ds(pl.multiple_of(step * SUB, SUB), SUB)
            own = lax.broadcasted_iota(jnp.int32, (SUB, strip), 0) + step * SUB
            for part in range(points // strip):
                columns = slice(part * strip, (part + 1) * strip)
                hit = jnp.where(own == order_ref[:, columns], 1.0, 0.0)
                pick[rows, columns] = hit.astype(BF)
                if part == 0:
                    pick8[rows, :strip] = hit.astype(F8)
                if part == points // strip - 1:
                    pick8[rows, strip:] = hit.astype(F8)
            placed = mm_nt(pick[rows, :], moved[...]).astype(BF)
            feat[rows, :] = placed[:, 2 * rank :]
            basis[rows, :] = placed[:, : 2 * rank]

        pl.semaphore_wait(barrier, len(devices))

    @pl.when(now < chunks)
    def _():
        rows = pl.ds(pl.multiple_of(now * chunk, chunk), chunk)
        block = [q_ref[pl.ds(tile, chunk, stride=tiles), :] for tile in range(tiles)]
        full, top, rest, unit = scaled(jnp.concatenate(block, axis=1))
        qh[rows, :] = top
        q8h[rows, :] = full.astype(F8)
        q8l[rows, :] = rest.astype(F8)
        unit_ref[rows, :] = jnp.broadcast_to(unit, (chunk, LANES))
        both = mm(top, basis[...])
        moment = (both[:, :rank] + both[:, rank:] + mm(rest.astype(BF), basis[:, :rank])) * unit
        share = row_count // low.size
        for part in range(chunk // share):
            packed[now * (chunk // share) + part] = pack(moment[part * share : (part + 1) * share])

    @pl.when(now == chunks)
    def _():
        low.send_up(packed)
        for copy in edges(row_count, PAD, chunks):
            copy.start()

    @pl.when(jnp.logical_and(now >= chunks, now < 2 * chunks))
    def _():
        part = now - chunks
        first = pl.multiple_of(part * chunk, chunk)
        rows = pl.ds(first, chunk)
        unit = unit_ref[rows, 0:1]
        for target, picked, picked8 in (
            (tail, slice(last, points), slice(strip, 2 * strip)),
            (head, slice(0, strip), slice(0, strip)),
        ):
            target[rows, :] = (
                mm(qh[rows, :], pick[:, picked]) + mm(q8l[rows, :], pick8[:, picked8])
            ) * unit
        for copy in edges(first, chunk, part):
            copy.start()

    @pl.when(now == 2 * chunks - 1)
    def _():
        low.levels(packed, transfer_ref, False)
        middle.send_up(low.top)

    def emit(rows, block, slot):
        total = mm(qh[rows, :], w[slot])
        total = total + mm(q8h[rows, :], w8l[slot])
        total = total + mm(q8l[rows, :], w8h[slot])
        out_ref[rows, block * SUB : (block + 1) * SUB] = total * unit_ref[rows, 0:1]

    @pl.when(now >= 2 * chunks)
    def _():
        sweep(feat, target, row_count, w, w8h, w8l, emit, 2, now - 2 * chunks)

    @pl.when(now == 2 * chunks)
    def _():
        middle.levels(low.top, transfer_ref, False)
        high.send_up(middle.top)

    @pl.when(now == 2 * chunks + 1)
    def _():
        high.levels(middle.top, transfer_ref, True)
        high.expand(None, transfer_ref, coupling_ref)
        middle.expand(high.chosen(), transfer_ref, coupling_ref)
        low.expand(middle.chosen(), transfer_ref, coupling_ref)
        low.send_down()

    @pl.when(now == pl.num_programs(0) - 1)
    def _():
        expansion_ref[...] = low.arrived()
        for copy in low.upward(packed) + low.downward():
            copy.wait_send()
        for copy in middle.upward(low.top) + high.upward(middle.top):
            copy.wait_send()
        for part in range(chunks):
            for copy in edges(part * chunk, chunk, part):
                copy.wait()
        for copy in edges(row_count, PAD, chunks):
            copy.wait()


def weight_scratch(count):
    return [
        pltpu.VMEM((2, count, SUB), BF),
        pltpu.VMEM((2, count, SUB), F8),
        pltpu.VMEM((2, count, SUB), F8),
    ]


def own_near(charges, order, jitter, bases, transfer, coupling):
    points = order.shape[1]
    tiles = points // LANES
    rows = charges.shape[0] // tiles
    strip = points // 4
    rank = bases.shape[0]
    chunk = 256
    chunks = rows // chunk
    leaf_bits = lax.axis_size("leaf").bit_length() - 1
    sub_bits = lax.axis_size("sub").bit_length() - 1
    near_bits = leaf_bits - leaf_bits // 2
    stages = [
        Stage("leaf", 0, near_bits, 0),
        Stage("leaf", near_bits, leaf_bits - near_bits, near_bits),
        Stage("sub", 0, sub_bits, leaf_bits),
    ]
    share = rows >> near_bits
    whole = lambda a: pl.BlockSpec(
        a.shape, lambda step: (0,) * len(a.shape), pipeline_mode=pl.Buffered(1)
    )
    fixed = lambda shape: pl.BlockSpec(shape, lambda step: (0,) * len(shape))
    far = pl.BlockSpec(memory_space=pl.ANY)
    scratch = []
    for stage in stages:
        scratch += stage.scratch(share, rank)
    shape = jax.ShapeDtypeStruct
    return pl.pallas_call(
        lambda *refs: own_kernel(stages, *refs),
        grid=(2 * chunks + points // (2 * SUB),),
        in_specs=[
            pl.BlockSpec((chunk * tiles, LANES), lambda step: (jnp.minimum(step, chunks - 1), 0))
        ]
        + [whole(a) for a in (order, jitter, bases, transfer, coupling)],
        out_specs=[
            pl.BlockSpec((rows, 2 * SUB), lambda step: (0, jnp.maximum(step - 2 * chunks, 0))),
            fixed((FEATS, points)),
            fixed((rows, rank)),
            far,
            far,
        ],
        out_shape=[
            shape((rows, points), F32),
            shape((FEATS, points), BF),
            shape((rows, rank), F32),
            shape((rows + PAD, strip), F32),
            shape((rows + PAD, strip), F32),
        ],
        scratch_shapes=[
            pltpu.VMEM((points, points), BF),
            pltpu.VMEM((points, 2 * strip), F8),
            pltpu.VMEM((points, 2 * rank), BF),
            pltpu.VMEM((2 * rank + FEATS, points), BF),
            pltpu.VMEM((FEATS, points), F32),
            pltpu.VMEM((FEATS, points), F32),
            pltpu.VMEM((points, FEATS), BF),
            pltpu.VMEM((FEATS, points), BF),
            pltpu.VMEM((rows, points), BF),
            pltpu.VMEM((rows, points), F8),
            pltpu.VMEM((rows, points), F8),
            pltpu.VMEM((rows, LANES), F32),
            pltpu.VMEM((rows + PAD, strip), F32),
            pltpu.VMEM((rows + PAD, strip), F32),
            pltpu.VMEM((1 << near_bits, share // 2, 2 * rank), F32),
            pltpu.SemaphoreType.DMA((4, chunks + 1)),
        ]
        + weight_scratch(points)
        + scratch,
        compiler_params=pltpu.CompilerParams(
            vmem_limit_bytes=LIMIT, collective_id=0, has_side_effects=True
        ),
        cost_estimate=pl.CostEstimate(
            flops=31_000_000_000, bytes_accessed=30_000_000, transcendentals=4_000_000
        ),
        name="own_near",
    )(charges, order, jitter, bases, transfer, coupling)


def rest_kernel(
    factor, left_ref, right_ref, edge_ref, target_ref, expansion_ref, bases_ref, near_ref,
    out_ref, qh, q8h, q8l, units, far, basis, source_rows, source, w, w8h, w8l,
):
    strip = left_ref.shape[1]
    rank = expansion_ref.shape[1]
    row_count = near_ref.shape[0]

    @pl.when(pl.program_id(0) == 0)
    def _():
        for ref, shift, columns in (
            (left_ref, -1.0, slice(0, strip)),
            (right_ref, 1.0, slice(strip, 2 * strip)),
        ):
            coords = [ref[row_count + axis : row_count + axis + 1, :] for axis in range(3)]
            coords[0] = coords[0] + shift / GAIN
            features(coords, source_rows, None, columns)
        source[...] = jnp.transpose(source_rows[...]).astype(BF)

        @pl.loop(0, row_count // SUB)
        def _(step):
            rows = pl.ds(pl.multiple_of(step * SUB, SUB), SUB)
            joined = jnp.concatenate(
                [left_ref[rows, :] * edge_ref[0:1, 0:1], right_ref[rows, :] * edge_ref[1:2, 0:1]],
                axis=1,
            )
            full, high, rest, unit = scaled(joined)
            qh[rows, :] = high
            q8h[rows, :] = full.astype(F8)
            q8l[rows, :] = rest.astype(F8)
            units[rows, :] = jnp.broadcast_to(unit, (SUB, units.shape[1]))
            top, low = split(expansion_ref[rows, :])
            far[rows, :rank] = top
            far[rows, rank : 2 * rank] = low.astype(BF)
            far[rows, 2 * rank :] = top

        top, low = split(bases_ref[...])
        basis[:rank, :] = top
        basis[rank : 2 * rank, :] = top
        basis[2 * rank :, :] = low.astype(BF)

    def emit(rows, block, slot):
        total = mm(qh[rows, :], w[slot])
        total = total + mm(q8h[rows, :], w8l[slot])
        total = total + mm(q8l[rows, :], w8h[slot])
        inner = slice(block * SUB, (block + 1) * SUB)
        total = total * units[rows, 0:1] + near_ref[rows, inner]
        columns = pl.ds(
            pl.multiple_of((pl.program_id(0) * OUT_BLOCKS + block) * SUB, SUB), SUB
        )
        total = total * factor + mm(far[rows, :], basis[:, columns])
        first = rows.start * PAD
        for part in range(SUB // LANES):
            place = first + block * (SUB // LANES) + part
            out_ref[pl.ds(place, rows.stop - rows.start, stride=PAD), :] = total[
                :, part * LANES : (part + 1) * LANES
            ]

    sweep(source, target_ref, row_count, w, w8h, w8l, emit, OUT_BLOCKS, pl.program_id(0))


def finish(left, right, edge, target, expansion, bases, near, factor):
    rows, points = near.shape
    strip = left.shape[1]
    rank = bases.shape[0]
    width = OUT_BLOCKS * SUB
    whole = lambda a: pl.BlockSpec(a.shape, lambda step: (0, 0), pipeline_mode=pl.Buffered(1))

    def kernel(*refs):
        out = refs[7]
        flat = out.reshape(rows * PAD, LANES)
        rest_kernel(factor, *refs[:7], flat, *refs[8:])

    return pl.pallas_call(
        kernel,
        grid=(points // width,),
        in_specs=[whole(a) for a in (left, right, edge, target, expansion, bases)]
        + [pl.BlockSpec((rows, width), lambda step: (0, step))],
        out_specs=pl.BlockSpec((rows, 1, PAD, LANES), lambda step: (0, step, 0, 0)),
        out_shape=jax.ShapeDtypeStruct((rows, points // width, PAD, LANES), F32),
        scratch_shapes=[
            pltpu.VMEM((rows, 2 * strip), BF),
            pltpu.VMEM((rows, 2 * strip), F8),
            pltpu.VMEM((rows, 2 * strip), F8),
            pltpu.VMEM((rows, LANES), F32),
            pltpu.VMEM((rows, 3 * rank), BF),
            pltpu.VMEM((3 * rank, points), BF),
            pltpu.VMEM((FEATS, 2 * strip), F32),
            pltpu.VMEM((2 * strip, FEATS), BF),
        ]
        + weight_scratch(2 * strip),
        compiler_params=pltpu.CompilerParams(vmem_limit_bytes=LIMIT),
        cost_estimate=pl.CostEstimate(
            flops=10_000_000_000, bytes_accessed=21_000_000, transcendentals=2_000_000
        ),
        name="finish",
    )(left, right, edge, target, expansion, bases, near)


def body(charges, ordering, jitter, leaf_bases, transfer, coupling):
    set_count, vector_count = (charges.shape[0], charges.shape[1])
    points = charges.shape[4]
    row_count = set_count * vector_count
    near_scale = points ** (-0.5)
    leaf_basis = leaf_bases.reshape(leaf_bases.shape[2], points)
    near_part, target_rows, expansion, left, right = own_near(
        charges.reshape(row_count * (points // LANES), LANES),
        ordering.reshape(1, points),
        jitter.reshape(3, 1, points),
        leaf_basis,
        transfer,
        coupling,
    )
    position = lax.axis_index("leaf")
    inner = jnp.stack([position > 0, position < lax.axis_size("leaf") - 1])
    edge = jnp.broadcast_to(inner[:, None].astype(F32), (2, LANES))
    potential = finish(
        left, right, edge, target_rows, expansion, leaf_basis, near_part, near_scale / GAIN
    )
    return potential.reshape(set_count, vector_count, 1, 1, points)


def solution(mesh):
    in_specs = (
        P(None, None, "sub", "leaf", None),
        P("sub", "leaf", None),
        P(None, "sub", "leaf", None),
        P("sub", "leaf", None, None),
        P(),
        P(),
    )
    out_specs = P(None, None, "sub", "leaf", None)
    return jax.shard_map(body, mesh=mesh, in_specs=in_specs, out_specs=out_specs, check_vma=False)
```

time: 105 us -> 89.9 us (0.86)
  Pallas kernels: 103 us -> 89.1 us
    pallas_call x2 -> x1, Pallas kernels: 83.5 us -> 68.9 us  [own_near(): pl.pallas_call(lambda *refs: own_kernel(stages, *refs), grid=(2 * chunks...]
where the time goes in v3:
time: 89.9 us; the launch traced here: 89.8 us
  Pallas kernels  89.1 us (99%)
    pallas_call x1, Pallas kernels, own_near(): pl.pallas_call(lambda *refs: own_kernel(stages, *refs), grid=(2 * chunks...  68.9 us
    pallas_call x1, Pallas kernels, finish(): pl.pallas_call(kernel, grid=(points // width,), in_specs=[whole(a) for a...  20.2 us

profile of v3, /device:TPU:1, one launch (start us, length us, event | category | flops | bytes accessed | tf_op | source)
XLA Modules:
  0.0 89.8 jit_solution(12311698233954447874)
XLA Ops:
  0.0 0.1 add_convert_fusion
  0.1 0.6 broadcast_in_dim.2.refs_2_
  0.7 68.9 %own_near.1 = (f32[1024,2048]{1,0:T(8,128)}, bf16[32,2048]{1,0:T(8,128)(2,1)}, f32[1024,64]{1,0:T(8,128)}, f32[1032,512]{1,0:T(8,128)}, f32[1032,512]{1,0:T(8,128)}) custom-call(f32[16384,128]{1,0:T(8,128)} %bitcast.7, s32[1,2048]{1,0:T(1,128)} %bitcast.11, f32[3,1,2048]{2,1,0:T(1,128)} %bitcast.10, f32[64,2048]{1,0:T(8,128)} %bitcast.8, ...), custom_call_target="tpu_custom_call" | custom-call | flops 31000000512 | bytes 30000000 | tf_op jit(solution)/shard_map/own_near/pallas_call | solution.py:446
  69.6 20.2 %finish.1 = f32[1024,2,8,128]{3,2,1,0:T(8,128)} custom-call(f32[1032,512]{1,0:T(8,128)} %get-tuple-element.10.refs_0_, f32[1032,512]{1,0:T(8,128)} %get-tuple-element.11.refs_1_, f32[2,128]{1,0:T(2,128)} %broadcast_in_dim.2.refs_2_, bf16[32,2048]{1,0:T(8,128)(2,1)} %get-tuple-element.12.refs_3_, f32[1024,64]{1,0:T(8,128)} %get-tuple-element.13.refs_4_, ...), custom_call_target="tpu_custom_call" | custom-call | flops 10000000000 | bytes 21000000 | tf_op jit(solution)/shard_map/finish/pallas_call | solution.py:570

commit v4 on v3

--- a/solution.py
+++ b/solution.py
@@ -348,8 +348,6 @@
     @pl.when(now == chunks)
     def _():
         low.send_up(packed)
-        for copy in edges(row_count, PAD, chunks):
-            copy.start()
 
     @pl.when(jnp.logical_and(now >= chunks, now < 2 * chunks))
     def _():
@@ -364,13 +362,21 @@
             target[rows, :] = (
                 mm(qh[rows, :], pick[:, picked]) + mm(q8l[rows, :], pick8[:, picked8])
             ) * unit
-        for copy in edges(first, chunk, part):
-            copy.start()
-
-    @pl.when(now == 2 * chunks - 1)
+
+    @pl.when(now == chunks + 1)
     def _():
         low.levels(packed, transfer_ref, False)
         middle.send_up(low.top)
+        for copy in edges(row_count, PAD, chunks):
+            copy.start()
+        for part in range(2):
+            for copy in edges(part * chunk, chunk, part):
+                copy.start()
+
+    @pl.when(now == 2 * chunks - 1)
+    def _():
+        middle.levels(low.top, transfer_ref, False)
+        high.send_up(middle.top)
 
     def emit(rows, block, slot):
         total = mm(qh[rows, :], w[slot])
@@ -384,16 +390,14 @@
 
     @pl.when(now == 2 * chunks)
     def _():
-        middle.levels(low.top, transfer_ref, False)
-        high.send_up(middle.top)
-
-    @pl.when(now == 2 * chunks + 1)
-    def _():
         high.levels(middle.top, transfer_ref, True)
         high.expand(None, transfer_ref, coupling_ref)
         middle.expand(high.chosen(), transfer_ref, coupling_ref)
         low.expand(middle.chosen(), transfer_ref, coupling_ref)
         low.send_down()
+        for part in range(2, chunks):
+            for copy in edges(part * chunk, chunk, part):
+                copy.start()
 
     @pl.when(now == pl.num_programs(0) - 1)
     def _():

time: 89.9 us -> 86.7 us (0.964)
  Pallas kernels: 89.1 us -> 85.9 us
    pallas_call x1, Pallas kernels: 68.9 us -> 65.7 us  [own_near(): pl.pallas_call(lambda *refs: own_kernel(stages, *refs), grid=(2 * chunks...]
where the time goes in v4:
time: 86.7 us; the launch traced here: 86.6 us
  Pallas kernels  85.9 us (99%)
    pallas_call x1, Pallas kernels, own_near(): pl.pallas_call(lambda *refs: own_kernel(stages, *refs), grid=(2 * chunks...  65.7 us
    pallas_call x1, Pallas kernels, finish(): pl.pallas_call(kernel, grid=(points // width,), in_specs=[whole(a) for a...  20.2 us

profile of v4, /device:TPU:1, one launch (start us, length us, event | category | flops | bytes accessed | tf_op | source)
XLA Modules:
  0.0 86.6 jit_solution(15691414429790639949)
XLA Ops:
  0.0 0.1 add_convert_fusion
  0.1 0.6 broadcast_in_dim.2.refs_2_
  0.7 65.7 %own_near.1 = (f32[1024,2048]{1,0:T(8,128)}, bf16[32,2048]{1,0:T(8,128)(2,1)}, f32[1024,64]{1,0:T(8,128)}, f32[1032,512]{1,0:T(8,128)}, f32[1032,512]{1,0:T(8,128)}) custom-call(f32[16384,128]{1,0:T(8,128)} %bitcast.7, s32[1,2048]{1,0:T(1,128)} %bitcast.11, f32[3,1,2048]{2,1,0:T(1,128)} %bitcast.10, f32[64,2048]{1,0:T(8,128)} %bitcast.8, ...), custom_call_target="tpu_custom_call" | custom-call | flops 31000000512 | bytes 30000000 | tf_op jit(solution)/shard_map/own_near/pallas_call | solution.py:450
  66.4 20.2 %finish.1 = f32[1024,2,8,128]{3,2,1,0:T(8,128)} custom-call(f32[1032,512]{1,0:T(8,128)} %get-tuple-element.10.refs_0_, f32[1032,512]{1,0:T(8,128)} %get-tuple-element.11.refs_1_, f32[2,128]{1,0:T(2,128)} %broadcast_in_dim.2.refs_2_, bf16[32,2048]{1,0:T(8,128)(2,1)} %get-tuple-element.12.refs_3_, f32[1024,64]{1,0:T(8,128)} %get-tuple-element.13.refs_4_, ...), custom_call_target="tpu_custom_call" | custom-call | flops 10000000000 | bytes 21000000 | tf_op jit(solution)/shard_map/finish/pallas_call | solution.py:574

commit v5 on v4

--- a/solution.py
+++ b/solution.py
@@ -369,7 +369,7 @@
         middle.send_up(low.top)
         for copy in edges(row_count, PAD, chunks):
             copy.start()
-        for part in range(2):
+        for part in range(0, 1):
             for copy in edges(part * chunk, chunk, part):
                 copy.start()
 
@@ -377,6 +377,9 @@
     def _():
         middle.levels(low.top, transfer_ref, False)
         high.send_up(middle.top)
+        for part in range(1, 2):
+            for copy in edges(part * chunk, chunk, part):
+                copy.start()
 
     def emit(rows, block, slot):
         total = mm(qh[rows, :], w[slot])

time: 86.7 us -> 86.7 us (level)
  no operation moved by 1% of the time
where the time goes in v5:
time: 86.7 us; the launch traced here: 86.6 us
  Pallas kernels  85.9 us (99%)
    pallas_call x1, Pallas kernels, own_near(): pl.pallas_call(lambda *refs: own_kernel(stages, *refs), grid=(2 * chunks...  65.8 us
    pallas_call x1, Pallas kernels, finish(): pl.pallas_call(kernel, grid=(points // width,), in_specs=[whole(a) for a...  20.2 us

profile of v5, /device:TPU:1, one launch (start us, length us, event | category | flops | bytes accessed | tf_op | source)
XLA Modules:
  0.0 86.6 jit_solution(15203261875316442096)
XLA Ops:
  0.0 0.1 add_convert_fusion
  0.1 0.6 broadcast_in_dim.2.refs_2_
  0.7 65.8 %own_near.1 = (f32[1024,2048]{1,0:T(8,128)}, bf16[32,2048]{1,0:T(8,128)(2,1)}, f32[1024,64]{1,0:T(8,128)}, f32[1032,512]{1,0:T(8,128)}, f32[1032,512]{1,0:T(8,128)}) custom-call(f32[16384,128]{1,0:T(8,128)} %bitcast.7, s32[1,2048]{1,0:T(1,128)} %bitcast.11, f32[3,1,2048]{2,1,0:T(1,128)} %bitcast.10, f32[64,2048]{1,0:T(8,128)} %bitcast.8, ...), custom_call_target="tpu_custom_call" | custom-call | flops 31000000512 | bytes 30000000 | tf_op jit(solution)/shard_map/own_near/pallas_call | solution.py:453
  66.5 20.2 %finish.1 = f32[1024,2,8,128]{3,2,1,0:T(8,128)} custom-call(f32[1032,512]{1,0:T(8,128)} %get-tuple-element.10.refs_0_, f32[1032,512]{1,0:T(8,128)} %get-tuple-element.11.refs_1_, f32[2,128]{1,0:T(2,128)} %broadcast_in_dim.2.refs_2_, bf16[32,2048]{1,0:T(8,128)(2,1)} %get-tuple-element.12.refs_3_, f32[1024,64]{1,0:T(8,128)} %get-tuple-element.13.refs_4_, ...), custom_call_target="tpu_custom_call" | custom-call | flops 10000000000 | bytes 21000000 | tf_op jit(solution)/shard_map/finish/pallas_call | solution.py:577
